TPU v7x, 32 devices: a whole 2x2x4 slice. The times are simulated.
32 devices in a mesh: batch: 2 (over y), seq: 4 (over x, core), kv: 4 (over z).
Axes of the slice: x: 2, y: 2, z: 4, core: 2. Of those that a mesh axis runs over, the one named last changes fastest.
Arguments:
- tokens: bfloat16 [4, 2048, 1536], P('batch', ('seq', 'kv')), may hold values from -6 to 6
- cotangent: bfloat16 [4, 2048, 1536], P('batch', ('seq', 'kv')), may hold values from -6 to 6
- segments: int32 [4, 2048], P('batch', 'seq'), may hold values from 0 to 2, as said below
- positions: int32 [4, 2048], P('batch', 'seq'), may hold values from 0 to 1535, as said below
- norm_in: float32 [1, 1536], P(None, ('batch', 'seq', 'kv')), may hold values from 0.5 to 1.5
- w_query: bfloat16 [1, 1536, 1536], P(None, ('batch', 'seq'), 'kv'), may hold values from -0.15625 to 0.15625
- w_key: bfloat16 [1, 1536, 768], P(None, ('batch', 'seq'), 'kv'), may hold values from -0.15625 to 0.15625
- w_value: bfloat16 [1, 1536, 768], P(None, ('batch', 'seq'), 'kv'), may hold values from -0.15625 to 0.15625
- w_out: bfloat16 [1, 1536, 1536], P(None, 'kv', ('batch', 'seq')), may hold values from -0.75 to 0.75
- norm_mid: float32 [1, 1536], P(None, ('batch', 'seq', 'kv')), may hold values from 0.5 to 1.5
- w_gate: bfloat16 [1, 1536, 4096], P(None, ('batch', 'seq'), 'kv'), may hold values from -0.15625 to 0.15625
- w_up: bfloat16 [1, 1536, 4096], P(None, ('batch', 'seq'), 'kv'), may hold values from -0.15625 to 0.15625
- w_down: bfloat16 [1, 4096, 1536], P(None, 'kv', ('batch', 'seq')), may hold values from -0.09375 to 0.09375
Outputs:
- out: float32 [4, 2048, 1536], P('batch', ('seq', 'kv'))
- grad_tokens: float32 [4, 2048, 1536], P('batch', ('seq', 'kv'))
- grad_norm_in: float32 [1, 1536], P(None, ('batch', 'seq', 'kv'))
- grad_w_query: float32 [1, 1536, 1536], P(None, ('batch', 'seq'), 'kv')
- grad_w_key: float32 [1, 1536, 768], P(None, ('batch', 'seq'), 'kv')
- grad_w_value: float32 [1, 1536, 768], P(None, ('batch', 'seq'), 'kv')
- grad_w_out: float32 [1, 1536, 1536], P(None, 'kv', ('batch', 'seq'))
- grad_norm_mid: float32 [1, 1536], P(None, ('batch', 'seq', 'kv'))
- grad_w_gate: float32 [1, 1536, 4096], P(None, ('batch', 'seq'), 'kv')
- grad_w_up: float32 [1, 1536, 4096], P(None, ('batch', 'seq'), 'kv')
- grad_w_down: float32 [1, 4096, 1536], P(None, 'kv', ('batch', 'seq'))
Inputs may be any that keep to these rules, and one draw needn't show every extreme that they name: `segments`: each row holds three documents with ids 0, 1, 2 in order; document 1 begins within the first 256 tokens of the row and is exactly 1536 tokens long, so document 2 begins within its last quarter. `positions`: the place of a token in its document, counted from 0.
All inputs are finite; a program needn't handle non-finite values.
Results may differ from a plain program's by a relative error of at most 0.02.
Values may be sent and summed in bfloat16 or wider, within the bound.
No kernel may reach another device: no remote copies, remote signals or barrier semaphores. Data moves between devices by JAX's collectives and lax.ppermute only.
A program may use at most 128 MiB of HBM per device.

v0:
```python
import functools
import math
from functools import partial

import jax
import jax.numpy as jnp
from jax import lax
from jax.experimental import pallas as pl
from jax.experimental.pallas import tpu as pltpu
from jax.sharding import Mesh
from jax.sharding import PartitionSpec as P

HD = 96
LAYERS = 1


EPS = 1e-05
THETA = 100000.0
BIG_NEG = -1e30


def rotary(positions_row):
    half_width = HD // 2
    frequency = THETA ** (-(2.0 * jnp.arange(half_width, dtype=jnp.float32)) / HD)
    angles = positions_row.astype(jnp.float32)[:, None] * frequency[None, :]
    cosine = jnp.concatenate([jnp.cos(angles), jnp.cos(angles)], axis=1)
    sine_table = jnp.concatenate([jnp.sin(angles), jnp.sin(angles)], axis=1)
    return (cosine, sine_table)


def rotate(head_vals, cosine, sine_table):
    half_width = head_vals.shape[-1] // 2
    swapped = jnp.concatenate([-head_vals[..., half_width:], head_vals[..., :half_width]], axis=-1)
    return head_vals * cosine[:, None, :] + swapped * sine_table[:, None, :]


def rms_norm(stream, gain):
    factor = lax.rsqrt(jnp.mean(stream * stream, axis=-1, keepdims=True) + EPS)
    return (stream * factor * gain, factor)


def norm_back(stream, factor, gain, upstream):
    scaled_grad = upstream * gain
    inner_mean = jnp.mean(scaled_grad * stream, axis=-1, keepdims=True)
    grad_stream = factor * scaled_grad - stream * factor**3 * inner_mean
    return (grad_stream, jnp.sum(upstream * stream * factor, axis=0))


def key_width(key_count):
    return math.gcd(key_count, 1024)


def contract(left_side, right_side, left_dim, right_dim):
    return lax.dot_general(
        left_side,
        right_side,
        (((left_dim,), (right_dim,)), ((), ())),
        preferred_element_type=jnp.float32,
    )


def spread(shard_rows):
    return lax.all_gather(shard_rows, "kv", axis=0, tiled=True)


def token_sum(pairs):
    summed = None
    for left_part, right_part, right_dim in pairs:
        product = contract(left_part, right_part, 1, right_dim)
        summed = product if summed is None else summed + product
    return lax.psum_scatter(
        summed.astype(jnp.bfloat16), "kv", scatter_dimension=0, tiled=True
    ).astype(jnp.float32)


def split_block(kv_both, seg_keys, offset, step_width, kv_local, head_size):
    kv_block = lax.dynamic_slice_in_dim(kv_both, offset, step_width, 0)
    key_block = kv_block[:, : kv_local * head_size].reshape(step_width, kv_local, head_size)
    value_block = kv_block[:, kv_local * head_size :].reshape(step_width, kv_local, head_size)
    seg_block = lax.dynamic_slice_in_dim(seg_keys, offset, step_width, 0)
    return (key_block, value_block, seg_block)


def forward_row(queries, seg_query, fold_state, kv_both, seg_keys, first_query, key_start):
    key_count = kv_both.shape[0]
    step_width = key_width(key_count)
    query_count, kv_local, group_size, head_size = queries.shape
    query_index = first_query + jnp.arange(query_count, dtype=jnp.int32)
    score_scale = head_size ** (-0.5)

    def forward_one_step(step_index, inner_state):
        running_max, weight_total, value_total = inner_state
        offset = step_index * step_width
        key_block, value_block, seg_block = split_block(
            kv_both, seg_keys, offset, step_width, kv_local, head_size
        )
        key_index = offset + jnp.arange(step_width, dtype=jnp.int32)
        allowed = (seg_query[:, None] == seg_block[None, :]) & (
            key_index[None, :] <= query_index[:, None]
        )
        scores = (
            jnp.einsum("qkgd,pkd->kgqp", queries, key_block, preferred_element_type=jnp.float32)
            * score_scale
        )
        scores = jnp.where(allowed, scores, BIG_NEG)
        new_max = jnp.maximum(running_max, jnp.max(scores, axis=-1))
        weights = jnp.where(allowed, jnp.exp(scores - new_max[..., None]), 0.0)
        rescale = jnp.exp(running_max - new_max)
        weight_total = rescale * weight_total + jnp.sum(weights, axis=-1)
        update = jnp.einsum(
            "kgqp,pkd->qkgd",
            weights.astype(jnp.bfloat16),
            value_block,
            preferred_element_type=jnp.float32,
        )
        value_total = jnp.transpose(rescale, (2, 0, 1))[..., None] * value_total + update
        return (new_max, weight_total, value_total)

    return lax.fori_loop(0, key_count // step_width, forward_one_step, fold_state)


def forward_fold(queries, seg_query, first_query, fold_state, pieces, key_start):
    kv_both, seg_keys = pieces
    row_fn = partial(forward_row, first_query=first_query, key_start=key_start)
    return jax.vmap(row_fn, in_axes=(0, 0, 0, 1, 1))(
        queries, seg_query, fold_state, kv_both, seg_keys
    )


def backward_row(
    queries,
    grad_attn,
    log_total,
    row_delta,
    seg_query,
    fold_state,
    kv_both,
    seg_keys,
    first_query,
    key_start,
):
    key_count = kv_both.shape[0]
    step_width = key_width(key_count)
    query_count, kv_local, group_size, head_size = queries.shape
    query_index = first_query + jnp.arange(query_count, dtype=jnp.int32)
    score_scale = head_size ** (-0.5)

    def backward_one_step(step_index, inner_state):
        grad_queries, grad_buffer = inner_state
        offset = step_index * step_width
        key_block, value_block, seg_block = split_block(
            kv_both, seg_keys, offset, step_width, kv_local, head_size
        )
        key_index = offset + jnp.arange(step_width, dtype=jnp.int32)
        allowed = (seg_query[:, None] == seg_block[None, :]) & (
            key_index[None, :] <= query_index[:, None]
        )
        scores = (
            jnp.einsum("qkgd,pkd->kgqp", queries, key_block, preferred_element_type=jnp.float32)
            * score_scale
        )
        probs_block = jnp.where(allowed, jnp.exp(scores - log_total[..., None]), 0.0)
        grad_probs = jnp.einsum(
            "qkgd,pkd->kgqp", grad_attn, value_block, preferred_element_type=jnp.float32
        )
        grad_scores = (probs_block * (grad_probs - row_delta[..., None])).astype(jnp.bfloat16)
        grad_queries = (
            grad_queries
            + jnp.einsum(
                "kgqp,pkd->qkgd", grad_scores, key_block, preferred_element_type=jnp.float32
            )
            * score_scale
        )
        grad_keys = (
            jnp.einsum("kgqp,qkgd->pkd", grad_scores, queries, preferred_element_type=jnp.float32)
            * score_scale
        )
        grad_values = jnp.einsum(
            "kgqp,qkgd->pkd",
            probs_block.astype(jnp.bfloat16),
            grad_attn,
            preferred_element_type=jnp.float32,
        )
        joined = jnp.concatenate(
            [grad_keys.reshape(step_width, -1), grad_values.reshape(step_width, -1)], axis=1
        )
        grad_buffer = lax.dynamic_update_slice_in_dim(grad_buffer, joined, offset, 0)
        return (grad_queries, grad_buffer)

    return lax.fori_loop(0, key_count // step_width, backward_one_step, fold_state)


def backward_fold(
    queries, grad_attn, log_total, row_delta, seg_query, first_query, fold_state, pieces, key_start
):
    kv_both, seg_keys = pieces
    row_fn = partial(backward_row, first_query=first_query, key_start=key_start)
    return jax.vmap(row_fn, in_axes=(0, 0, 0, 0, 0, 0, 1, 1))(
        queries, grad_attn, log_total, row_delta, seg_query, fold_state, kv_both, seg_keys
    )


def layer_forward(stream, gain_pair, matrices, seg_info, tables):
    gain_in, gain_mid = gain_pair
    w_query, w_key, w_value, w_out, w_gate, w_up, w_down = matrices
    seg_query, seg_keys = seg_info
    cosine, sine_table = tables
    row_count = seg_query.shape[0]
    kv_local = w_key.shape[1] // HD
    head_local = w_query.shape[1] // HD
    group_size = head_local // kv_local
    normed_a, factor_a = rms_norm(stream, gain_in)
    spread_a = spread(normed_a.astype(jnp.bfloat16))
    flat_count = spread_a.shape[0]
    token_count = flat_count // row_count
    raw_queries = jnp.dot(spread_a, w_query, preferred_element_type=jnp.float32).reshape(
        flat_count, head_local, HD
    )
    queries = (
        rotate(raw_queries, cosine, sine_table)
        .astype(jnp.bfloat16)
        .reshape(token_count, row_count, kv_local, group_size, HD)
    )
    queries = jnp.transpose(queries, (1, 0, 2, 3, 4))
    raw_keys = jnp.dot(spread_a, w_key, preferred_element_type=jnp.float32).reshape(
        flat_count, kv_local, HD
    )
    keys_low = (
        rotate(raw_keys, cosine, sine_table).astype(jnp.bfloat16).reshape(flat_count, kv_local * HD)
    )
    values_low = jnp.dot(spread_a, w_value, preferred_element_type=jnp.float32).astype(jnp.bfloat16)
    kv_both = jnp.concatenate([keys_low, values_low], axis=1).reshape(
        token_count, row_count, 2 * kv_local * HD
    )
    first_query = lax.axis_index("seq") * token_count
    start_state = (
        jnp.full((row_count, kv_local, group_size, token_count), BIG_NEG, jnp.float32),
        jnp.zeros((row_count, kv_local, group_size, token_count), jnp.float32),
        jnp.zeros((row_count, token_count, kv_local, group_size, HD), jnp.float32),
    )
    running_max, weight_total, value_total = forward_fold(
        queries,
        seg_query,
        first_query,
        start_state,
        (
            lax.all_gather(kv_both, "seq", axis=0, tiled=True),
            lax.all_gather(seg_keys, "seq", axis=0, tiled=True),
        ),
        jnp.int32(0),
    )
    attn_float = value_total / jnp.transpose(weight_total, (0, 3, 1, 2))[..., None]
    log_total = running_max + jnp.log(weight_total)
    attn_low = (
        jnp.transpose(attn_float, (1, 0, 2, 3, 4))
        .reshape(flat_count, head_local * HD)
        .astype(jnp.bfloat16)
    )
    stream_mid = stream + token_sum(((attn_low, w_out, 0),))
    normed_b, factor_b = rms_norm(stream_mid, gain_mid)
    spread_b = spread(normed_b.astype(jnp.bfloat16))
    gate_val = jnp.dot(spread_b, w_gate, preferred_element_type=jnp.float32)
    up_val = jnp.dot(spread_b, w_up, preferred_element_type=jnp.float32)
    hidden = (jax.nn.silu(gate_val) * up_val).astype(jnp.bfloat16)
    stream_out = stream_mid + token_sum(((hidden, w_down, 0),))
    saved_state = (
        stream,
        factor_a,
        spread_a,
        queries,
        kv_both,
        attn_float,
        attn_low,
        log_total,
        stream_mid,
        factor_b,
        spread_b,
        gate_val,
        up_val,
        hidden,
    )
    return (stream_out, saved_state)


def layer_backward(saved_state, grad_stream, gain_pair, matrices, seg_info, tables):
    (
        stream,
        factor_a,
        spread_a,
        queries,
        kv_both,
        attn_float,
        attn_low,
        log_total,
        stream_mid,
        factor_b,
        spread_b,
        gate_val,
        up_val,
        hidden,
    ) = saved_state
    gain_in, gain_mid = gain_pair
    w_query, w_key, w_value, w_out, w_gate, w_up, w_down = matrices
    seg_query, seg_keys = seg_info
    cosine, sine_table = tables
    row_count, token_count, kv_local, group_size, head_size = queries.shape
    head_local = kv_local * group_size
    flat_count = row_count * token_count
    grad_low = spread(grad_stream.astype(jnp.bfloat16))
    grad_down_w = contract(hidden, grad_low, 0, 0)
    grad_hidden = contract(grad_low, w_down, 1, 1)
    sigmoid_gate = jax.nn.sigmoid(gate_val)
    silu_gate = gate_val * sigmoid_gate
    grad_gate_low = (
        grad_hidden * up_val * sigmoid_gate * (1.0 + gate_val * (1.0 - sigmoid_gate))
    ).astype(jnp.bfloat16)
    grad_up_low = (grad_hidden * silu_gate).astype(jnp.bfloat16)
    grad_gate_w = contract(spread_b, grad_gate_low, 0, 0)
    grad_up_w = contract(spread_b, grad_up_low, 0, 0)
    grad_normed_b = token_sum(((grad_gate_low, w_gate, 1), (grad_up_low, w_up, 1)))
    back_mid, grad_gain_mid = norm_back(stream_mid, factor_b, gain_mid, grad_normed_b)
    grad_mid = grad_stream + back_mid
    grad_attn_full = spread(grad_mid.astype(jnp.bfloat16))
    grad_out_w = contract(attn_low, grad_attn_full, 0, 0)
    grad_attn = (
        contract(grad_attn_full, w_out, 1, 1)
        .astype(jnp.bfloat16)
        .reshape(token_count, row_count, kv_local, group_size, head_size)
    )
    grad_attn = jnp.transpose(grad_attn, (1, 0, 2, 3, 4))
    row_delta = jnp.transpose(jnp.sum(grad_attn * attn_float, axis=-1), (0, 2, 3, 1))
    first_query = lax.axis_index("seq") * token_count
    row_length = token_count * lax.axis_size("seq")
    start_state = (
        jnp.zeros((row_count, token_count, kv_local, group_size, head_size), jnp.float32),
        jnp.zeros((row_count, row_length, 2 * kv_local * head_size), jnp.float32),
    )
    grad_queries, grad_buffer = backward_fold(
        queries,
        grad_attn,
        log_total,
        row_delta,
        seg_query,
        first_query,
        start_state,
        (
            lax.all_gather(kv_both, "seq", axis=0, tiled=True),
            lax.all_gather(seg_keys, "seq", axis=0, tiled=True),
        ),
        jnp.int32(0),
    )
    grad_kv = lax.psum_scatter(
        grad_buffer.astype(jnp.bfloat16), "seq", scatter_dimension=1, tiled=True
    ).astype(jnp.float32)
    grad_kv = jnp.transpose(grad_kv, (1, 0, 2)).reshape(flat_count, 2 * kv_local * head_size)
    grad_queries = jnp.transpose(grad_queries, (1, 0, 2, 3, 4)).reshape(
        flat_count, head_local, head_size
    )
    grad_q_low = (
        rotate(grad_queries, cosine, -sine_table)
        .astype(jnp.bfloat16)
        .reshape(flat_count, head_local * head_size)
    )
    grad_k_low = (
        rotate(
            grad_kv[:, : kv_local * head_size].reshape(flat_count, kv_local, head_size),
            cosine,
            -sine_table,
        )
        .astype(jnp.bfloat16)
        .reshape(flat_count, kv_local * head_size)
    )
    grad_v_low = grad_kv[:, kv_local * head_size :].astype(jnp.bfloat16)
    grad_query_w = contract(spread_a, grad_q_low, 0, 0)
    grad_key_w = contract(spread_a, grad_k_low, 0, 0)
    grad_value_w = contract(spread_a, grad_v_low, 0, 0)
    grad_normed_a = token_sum(
        ((grad_q_low, w_query, 1), (grad_k_low, w_key, 1), (grad_v_low, w_value, 1))
    )
    back_in, grad_gain_in = norm_back(stream, factor_a, gain_in, grad_normed_a)
    grad_input = grad_mid + back_in
    weight_grads = (
        lax.psum_scatter(
            grad_query_w.astype(jnp.bfloat16), ("batch", "seq"), scatter_dimension=0, tiled=True
        ).astype(jnp.float32),
        lax.psum_scatter(
            grad_key_w.astype(jnp.bfloat16), ("batch", "seq"), scatter_dimension=0, tiled=True
        ).astype(jnp.float32),
        lax.psum_scatter(
            grad_value_w.astype(jnp.bfloat16), ("batch", "seq"), scatter_dimension=0, tiled=True
        ).astype(jnp.float32),
        lax.psum_scatter(
            grad_out_w.astype(jnp.bfloat16), ("batch", "seq"), scatter_dimension=1, tiled=True
        ).astype(jnp.float32),
        lax.psum_scatter(
            grad_gate_w.astype(jnp.bfloat16), ("batch", "seq"), scatter_dimension=0, tiled=True
        ).astype(jnp.float32),
        lax.psum_scatter(
            grad_up_w.astype(jnp.bfloat16), ("batch", "seq"), scatter_dimension=0, tiled=True
        ).astype(jnp.float32),
        lax.psum_scatter(
            grad_down_w.astype(jnp.bfloat16), ("batch", "seq"), scatter_dimension=1, tiled=True
        ).astype(jnp.float32),
    )
    return (grad_input, weight_grads, grad_gain_in, grad_gain_mid)


def to_flat(shard_rows):
    row_count, token_part, width = shard_rows.shape
    return jnp.transpose(shard_rows.astype(jnp.float32), (1, 0, 2)).reshape(
        token_part * row_count, width
    )


def from_flat(flat_rows, row_count):
    token_part = flat_rows.shape[0] // row_count
    return jnp.transpose(flat_rows.reshape(token_part, row_count, flat_rows.shape[1]), (1, 0, 2))


def general_local(
    tokens,
    cotangent,
    segments,
    positions,
    norm_in,
    w_query,
    w_key,
    w_value,
    w_out,
    norm_mid,
    w_gate,
    w_up,
    w_down,
):
    gains_in, gains_mid = (
        lax.all_gather(norm_in, ("batch", "seq", "kv"), axis=1, tiled=True),
        lax.all_gather(norm_mid, ("batch", "seq", "kv"), axis=1, tiled=True),
    )
    row_count = tokens.shape[0]
    seg_info = (segments, jnp.transpose(segments, (1, 0)))
    tables = rotary(jnp.transpose(positions, (1, 0)).reshape(-1))

    def fetch_layer(layer_index):
        return (
            lax.all_gather(w_query[layer_index], ("batch", "seq"), axis=0, tiled=True),
            lax.all_gather(w_key[layer_index], ("batch", "seq"), axis=0, tiled=True),
            lax.all_gather(w_value[layer_index], ("batch", "seq"), axis=0, tiled=True),
            lax.all_gather(w_out[layer_index], ("batch", "seq"), axis=1, tiled=True),
            lax.all_gather(w_gate[layer_index], ("batch", "seq"), axis=0, tiled=True),
            lax.all_gather(w_up[layer_index], ("batch", "seq"), axis=0, tiled=True),
            lax.all_gather(w_down[layer_index], ("batch", "seq"), axis=1, tiled=True),
        )

    stream = to_flat(tokens)
    fetched = []
    states = []
    layer_index = 0
    matrices = fetch_layer(layer_index)
    layer_inputs = [stream]
    stream, saved_state = layer_forward(
        stream, (gains_in[layer_index], gains_mid[layer_index]), matrices, seg_info, tables
    )
    fetched.append(matrices)
    states.append(saved_state)
    grad_stream = to_flat(cotangent)
    grads_in = []
    grads_mid = []
    weight_lists = []
    for layer_index in reversed(range(LAYERS)):
        gain_pair = (gains_in[layer_index], gains_mid[layer_index])
        matrices = fetch_layer(layer_index)
        saved_state = layer_forward(
            layer_inputs[layer_index], gain_pair, matrices, seg_info, tables
        )[1]
        grad_stream, weight_grads, grad_gain_in, grad_gain_mid = layer_backward(
            saved_state, grad_stream, gain_pair, matrices, seg_info, tables
        )
        grads_in.insert(0, grad_gain_in)
        grads_mid.insert(0, grad_gain_mid)
        weight_lists.insert(0, weight_grads)
    gain_grads_in, gain_grads_mid = (
        lax.psum_scatter(
            jnp.stack(grads_in), ("batch", "seq", "kv"), scatter_dimension=1, tiled=True
        ),
        lax.psum_scatter(
            jnp.stack(grads_mid), ("batch", "seq", "kv"), scatter_dimension=1, tiled=True
        ),
    )
    stacked_grads = [
        jnp.stack([grad_set[member] for grad_set in weight_lists]) for member in range(7)
    ]
    return (
        from_flat(stream, row_count),
        from_flat(grad_stream, row_count),
        gain_grads_in,
        stacked_grads[0],
        stacked_grads[1],
        stacked_grads[2],
        stacked_grads[3],
        gain_grads_mid,
        stacked_grads[4],
        stacked_grads[5],
        stacked_grads[6],
    )


def general_solution(mesh):
    in_specs = (
        P("batch", ("seq", "kv"), None),
        P("batch", ("seq", "kv"), None),
        P("batch", "seq"),
        P("batch", "seq"),
        P(None, ("batch", "seq", "kv")),
        P(None, ("batch", "seq"), "kv"),
        P(None, ("batch", "seq"), "kv"),
        P(None, ("batch", "seq"), "kv"),
        P(None, "kv", ("batch", "seq")),
        P(None, ("batch", "seq", "kv")),
        P(None, ("batch", "seq"), "kv"),
        P(None, ("batch", "seq"), "kv"),
        P(None, "kv", ("batch", "seq")),
    )
    out_specs = (
        P("batch", ("seq", "kv"), None),
        P("batch", ("seq", "kv"), None),
        P(None, ("batch", "seq", "kv")),
        P(None, ("batch", "seq"), "kv"),
        P(None, ("batch", "seq"), "kv"),
        P(None, ("batch", "seq"), "kv"),
        P(None, "kv", ("batch", "seq")),
        P(None, ("batch", "seq", "kv")),
        P(None, ("batch", "seq"), "kv"),
        P(None, ("batch", "seq"), "kv"),
        P(None, "kv", ("batch", "seq")),
    )
    return jax.shard_map(general_local, mesh=mesh, in_specs=in_specs, out_specs=out_specs, check_vma=False)


LN = 128
NEG=-1e30
C2 = (96 ** -0.5) * 1.4426950408889634

def cost(microseconds):
    return pl.CostEstimate(
        flops=microseconds * 10**9, bytes_accessed=microseconds * 3 * 10**6, transcendentals=0
    )


def lane_iota(rows):
    return lax.broadcasted_iota(jnp.int32, (rows, LN), 1)

def unpack4(t0, t1, t2):
    lane = lane_iota(t0.shape[0])
    live = lane < HD
    zero = jnp.zeros_like(t0)
    a = t0
    b = pltpu.roll(jnp.where(lane >= 96, t0, t1), 32, 1)
    c = pltpu.roll(jnp.where(lane >= 64, t1, t2), 64, 1)
    d = pltpu.roll(t2, 96, 1)
    return tuple(jnp.where(live, v, zero) for v in (a, b, c, d))

def pack4(a, b, c, d):
    lane = lane_iota(a.shape[0])
    b, c, d = pltpu.roll(b, 96, 1), pltpu.roll(c, 64, 1), pltpu.roll(d, 32, 1)
    return (jnp.where(lane < 96, a, b), jnp.where(lane < 64, b, c), jnp.where(lane < 32, c, d))

def split3(x):
    x = x.astype(jnp.float32)
    return x[:, :LN], x[:, LN:2*LN], x[:, 2*LN:]

def doc_low(index, first, length):
    second = first + 3 * length // 4
    return jnp.where(index >= second, second, jnp.where(index >= first, first, 0))

BQ = 256
BK = 512

def dotf(a, b, dims):
    return lax.dot_general(a, b, (dims, ((), ())), preferred_element_type=jnp.float32)

def attn_fwd_kernel(length, first_ref, x_ref, o_ref, of_ref, lse_ref, q_s, k_s, v_s, s_s):
    i = pl.program_id(0)
    blocks = length // BQ
    first = first_ref[0]

    @pl.when(i == 0)
    def _():
        def body(j, carry):
            rows = pl.ds(pl.multiple_of(j * BQ, BQ), BQ)
            q0, q1, k, v = unpack4(*split3(x_ref[rows, :]))
            q_s[j, :BQ, :] = q0.astype(jnp.bfloat16)
            q_s[j, BQ:, :] = q1.astype(jnp.bfloat16)
            k_s[rows, :] = k.astype(jnp.bfloat16)
            v_s[rows, :] = v.astype(jnp.bfloat16)
            return carry

        lax.fori_loop(0, blocks, body, 0)

    q = q_s[i]
    late = (3 * length // 4 + length // 8) // BQ
    start = jnp.where(i >= late, 3 * length // 4 // BK, 0)
    stop = i * BQ // BK + 1
    q_index = i * BQ + lax.broadcasted_iota(jnp.int32, (BQ, 1), 0)
    low = doc_low(q_index, first, length)

    def fold(v, op):
        out = v[:, :LN]
        for n in range(1, BK // LN):
            out = op(out, v[:, n * LN : (n + 1) * LN])
        return out

    def score(j, top):
        s = dotf(q, k_s[pl.ds(pl.multiple_of(j * BK, BK), BK), :], ((1,), (1,)))
        key = j * BK + lax.broadcasted_iota(jnp.int32, (1, BK), 1)
        ok = (key <= q_index) & (key >= low)
        s = jnp.concatenate([jnp.where(ok, s[:BQ], NEG), jnp.where(ok, s[BQ:], NEG)], axis=0)
        s_s[j] = s
        return jnp.maximum(top, fold(s, jnp.maximum))

    top = lax.fori_loop(start, stop, score, jnp.full((2 * BQ, LN), NEG, jnp.float32))
    m = jnp.max(top, axis=1, keepdims=True) * C2

    def add(j, state):
        p = jnp.exp2(s_s[j] * C2 - m)
        keys = pl.ds(pl.multiple_of(j * BK, BK), BK)
        of_ref[0] += dotf(p.astype(jnp.bfloat16), v_s[keys, :], ((1,), (0,)))
        return state + fold(p, jnp.add)

    zero = jnp.zeros((2 * BQ, LN), jnp.float32)
    of_ref[0] = zero
    total = lax.fori_loop(start, stop, add, zero)
    total = jnp.sum(total, axis=1, keepdims=True)
    out = of_ref[0] / total
    lse = jnp.broadcast_to(m + jnp.log2(total), (2 * BQ, LN))
    lse_ref[0] = jnp.transpose(lse, (1, 0))[:8, :]
    of_ref[0] = out
    for d in range(2):
        at = d * 128
        parts = [out[at + n // 2 * 64 + n % 2 * BQ : at + n // 2 * 64 + n % 2 * BQ + 64] for n in range(4)]
        for n, t in enumerate(pack4(*parts)):
            o_ref[d, :, n * LN : (n + 1) * LN] = t.astype(jnp.bfloat16)


def attn_fwd(first, x):
    length = x.shape[0]
    blocks = length // BQ
    return pl.pallas_call(
        functools.partial(attn_fwd_kernel, length),
        grid=(blocks,),
        in_specs=[pl.BlockSpec(memory_space=pltpu.SMEM),
                  pl.BlockSpec((length, 3*LN), lambda i: (0, 0))],
        out_specs=[pl.BlockSpec((2, 64, 3*LN), lambda i: (i, 0, 0)),
                   pl.BlockSpec((1, 2*BQ, LN), lambda i: (i, 0, 0)),
                   pl.BlockSpec((1, 8, 2*BQ), lambda i: (i, 0, 0))],
        out_shape=[jax.ShapeDtypeStruct((length//128, 64, 3*LN), jnp.bfloat16),
                   jax.ShapeDtypeStruct((blocks, 2*BQ, LN), jnp.float32),
                   jax.ShapeDtypeStruct((blocks, 8, 2*BQ), jnp.float32)],
        scratch_shapes=[pltpu.VMEM((blocks, 2*BQ, LN), jnp.bfloat16),
                        pltpu.VMEM((length, LN), jnp.bfloat16),
                        pltpu.VMEM((length, LN), jnp.bfloat16),
                        pltpu.VMEM((length // BK, 2*BQ, BK), jnp.float32)],
        compiler_params=pltpu.CompilerParams(vmem_limit_bytes=48 << 20),
        name="attend",
        cost_estimate=cost(22),
    )(first, x)

def attn_bwd_kernel(length, first_ref, x_ref, do_ref, of_ref, lse_ref, cos_ref, sin_ref, out_ref,
                    q_s, k_s, v_s, do_s, dl_s, dq_s, dk_s, dv_s):
    j = pl.program_id(0)
    blocks = length // BQ
    first = first_ref[0]
    @pl.when(j == 0)
    def _():
        def body(b, carry):
            rows = pl.ds(pl.multiple_of(b * BQ, BQ), BQ)
            q0, q1, k, v = unpack4(*split3(x_ref[rows, :]))
            q_s[b, :BQ, :] = q0.astype(jnp.bfloat16)
            q_s[b, BQ:, :] = q1.astype(jnp.bfloat16)
            k_s[b] = k.astype(jnp.bfloat16)
            v_s[b] = v.astype(jnp.bfloat16)
            for d in range(2):
                parts = unpack4(*split3(do_ref[2*b + d]))
                for n, part in enumerate(parts):
                    at = (n % 2) * BQ + d*128 + (n // 2) * 64
                    do_s[b, at:at+64, :] = part.astype(jnp.bfloat16)
            prod = do_s[b].astype(jnp.float32) * of_ref[b]
            delta = jnp.broadcast_to(jnp.sum(prod, axis=1, keepdims=True), (2*BQ, LN))
            dl_s[b] = jnp.transpose(delta, (1, 0))[:8, :]
            dq_s[b] = jnp.zeros((2*BQ, LN), jnp.float32)
            return carry
        lax.fori_loop(0, blocks, body, 0)
    late = (3 * length // 4 + length // 8) // BQ
    third = 3 * length // 4 // BQ
    stop = jnp.where(j >= third, blocks, late)
    k = k_s[j]
    v = v_s[j]
    dk_s[j] = jnp.zeros((BQ, LN), jnp.float32)
    dv_s[j] = jnp.zeros((BQ, LN), jnp.float32)
    key = j * BQ + lax.broadcasted_iota(jnp.int32, (BQ, 1), 0)

    def steps(places):
        dk, dv = [], []
        for i in places:
            q, do = q_s[i], do_s[i]
            s = dotf(k, q, ((1,), (1,)))
            dp = dotf(v, do, ((1,), (1,)))
            q_index = i * BQ + lax.broadcasted_iota(jnp.int32, (1, BQ), 1)
            ok = (key <= q_index) & (key >= doc_low(q_index, first, length))
            p = jnp.exp2(s * C2 - lse_ref[i, 0:1, :])
            p = jnp.concatenate([jnp.where(ok, p[:, :BQ], 0.0), jnp.where(ok, p[:, BQ:], 0.0)], axis=1)
            ds = (p * (dp - dl_s[i, 0:1, :])).astype(jnp.bfloat16)
            dv.append(dotf(p.astype(jnp.bfloat16), do, ((1,), (0,))))
            dk.append(dotf(ds, q, ((1,), (0,))))
            dq_s[i] += dotf(ds, k, ((0,), (0,)))
        dv_s[j] += functools.reduce(jnp.add, dv)
        dk_s[j] += functools.reduce(jnp.add, dk)

    pairs = (stop - j) // 2

    def body(n, carry):
        steps((j + 2 * n, j + 2 * n + 1))
        return carry

    lax.fori_loop(0, pairs, body, 0)

    @pl.when(j + 2 * pairs < stop)
    def _():
        steps((stop - 1,))

    @pl.when(j == blocks - 1)
    def _():
        scale = HD ** -0.5
        lower = lane_iota(BQ) < HD // 2

        def turn_back(piece, cosine, sine):
            swapped = jnp.where(lower, -pltpu.roll(piece, LN - HD // 2, 1), pltpu.roll(piece, HD // 2, 1))
            return (piece * cosine - swapped * sine) * scale

        def body(b, carry):
            rows = pl.ds(pl.multiple_of(b * BQ, BQ), BQ)
            cosine, sine = cos_ref[rows, :], sin_ref[rows, :]
            pieces = [turn_back(v, cosine, sine) for v in (dq_s[b, :BQ, :], dq_s[b, BQ:, :], dk_s[b])]
            for n, tile in enumerate(pack4(*pieces, dv_s[b])):
                out_ref[rows, n * LN : (n + 1) * LN] = tile.astype(jnp.bfloat16)
            return carry

        lax.fori_loop(0, blocks, body, 0)


def attn_bwd(first, x, do, of, lse, cos, sin):
    length = x.shape[0]
    blocks = length // BQ
    whole = lambda a: pl.BlockSpec(a.shape, lambda j: (0,) * a.ndim)
    return pl.pallas_call(
        functools.partial(attn_bwd_kernel, length),
        grid=(blocks,),
        in_specs=[pl.BlockSpec(memory_space=pltpu.SMEM)] + [whole(a) for a in (x, do, of, lse, cos, sin)],
        out_specs=pl.BlockSpec((length, 3*LN), lambda j: (0, 0)),
        out_shape=jax.ShapeDtypeStruct((length, 3*LN), jnp.bfloat16),
        scratch_shapes=[pltpu.VMEM((blocks, 2*BQ, LN), jnp.bfloat16),
                        pltpu.VMEM((blocks, BQ, LN), jnp.bfloat16),
                        pltpu.VMEM((blocks, BQ, LN), jnp.bfloat16),
                        pltpu.VMEM((blocks, 2*BQ, LN), jnp.bfloat16),
                        pltpu.VMEM((blocks, 8, 2*BQ), jnp.float32),
                        pltpu.VMEM((blocks, 2*BQ, LN), jnp.float32),
                        pltpu.VMEM((blocks, BQ, LN), jnp.float32),
                        pltpu.VMEM((blocks, BQ, LN), jnp.float32)],
        compiler_params=pltpu.CompilerParams(vmem_limit_bytes=56 << 20),
        name="attend_back",
        cost_estimate=cost(31),
    )(first, x, do, of, lse, cos, sin)


def widen(table):
    lane = lane_iota(table.shape[0])
    second = jnp.where(lane < 96, pltpu.roll(table, 96, 1), pltpu.roll(table, 16, 1))
    third = jnp.where(lane < 112, pltpu.roll(table, 112, 1), pltpu.roll(table, 32, 1))
    return second, third


def cos_sin3(cos, sin):
    lane = lane_iota(cos.shape[0])
    live = lane < 32
    cos_two, cos_three = widen(cos)
    sin_two, sin_three = widen(sin)
    cosine = jnp.concatenate([cos, cos_two, jnp.where(live, cos_three, 1.0)], axis=1)
    lower = (
        (lane < 48) | (lane >= 96),
        (lane < 16) | ((lane >= 64) & (lane < 112)),
        (lane >= 32) & (lane < 80),
    )
    tiles = (sin, sin_two, jnp.where(live, sin_three, 0.0))
    sine = jnp.concatenate([jnp.where(l, -t, t) for l, t in zip(lower, tiles)], axis=1)
    return cosine, sine, lower


def turn(values, cosine, sine, lower):
    width = values.shape[1]
    left, right = pltpu.roll(values, width - HD // 2, 1), pltpu.roll(values, HD // 2, 1)
    swapped = [
        jnp.where(l, left[:, n * LN : (n + 1) * LN], right[:, n * LN : (n + 1) * LN])
        for n, l in enumerate(lower)
    ]
    return values * cosine + jnp.concatenate(swapped, axis=1) * sine


def full_spec(array):
    rank = array.ndim
    return pl.BlockSpec(array.shape, lambda *_: (0,) * rank)


def qkv_kernel(parts, rows, h_ref, gain_ref, w_ref, cos_ref, sin_ref, a_ref, out_ref):
    count = h_ref.shape[0] // parts
    tokens = count // rows

    def body(z, carry):
        stream = h_ref[pl.ds(pl.multiple_of(z * count, count), count), :].astype(jnp.float32)
        factor = lax.rsqrt(jnp.mean(stream * stream, axis=-1, keepdims=True) + EPS)
        normed = (stream * factor * gain_ref[...]).astype(jnp.bfloat16)
        at = pl.ds(pl.multiple_of(z * tokens, tokens), tokens)
        for r in range(rows):
            a_ref[r, at, :] = normed[r * tokens : (r + 1) * tokens]
        product = dotf(normed, w_ref[...], ((1,), (0,)))
        for r in range(rows):
            cosine, sine, lower = cos_sin3(cos_ref[r, at, :], sin_ref[r, at, :])
            for h in range(product.shape[1] // (3 * LN)):
                piece = product[r * tokens : (r + 1) * tokens, h * 3 * LN : (h + 1) * 3 * LN]
                out_ref[h * rows + r, at, :] = turn(piece, cosine, sine, lower).astype(jnp.bfloat16)
        return carry

    lax.fori_loop(0, parts, body, 0)


def qkv_call(parts, group, gain, weight, cos, sin, rows):
    count, width = group.shape
    tokens = count // rows
    groups = weight.shape[1] // (3 * LN)
    operands = (group, gain, weight, cos, sin)
    return pl.pallas_call(
        partial(qkv_kernel, parts, rows),
        grid=(1,),
        in_specs=[full_spec(v) for v in operands],
        out_specs=[
            pl.BlockSpec((rows, tokens, width), lambda i: (0, 0, 0)),
            pl.BlockSpec((groups * rows, tokens, 3 * LN), lambda i: (0, 0, 0)),
        ],
        out_shape=[
            jax.ShapeDtypeStruct((rows, tokens, width), jnp.bfloat16),
            jax.ShapeDtypeStruct((groups * rows, tokens, 3 * LN), jnp.bfloat16),
        ],
        compiler_params=pltpu.CompilerParams(vmem_limit_bytes=48 << 20),
        name="norm_qkv",
        cost_estimate=cost(7),
    )(*operands)


def thirds(values):
    return values[:, :LN], values[:, LN : 2 * LN], values[:, 2 * LN :]


def join_pairs(left, right):
    l0, l1, l2 = thirds(left)
    r0, r1, r2 = thirds(right)
    low = lane_iota(left.shape[0]) < 64
    s0, s1, s2 = (pltpu.roll(v, 64, 1) for v in (r0, r1, r2))
    firsts = (l0, jnp.where(low, l1, s0), jnp.where(low, s0, s1))
    m1, m2 = pltpu.roll(l1, 64, 1), pltpu.roll(l2, 64, 1)
    lasts = (jnp.where(low, m1, m2), jnp.where(low, m2, r1), r2)
    return jnp.concatenate(firsts, axis=1), jnp.concatenate(lasts, axis=1)


def out_kernel(rows, parts, o_ref, w_ref, tok_ref, gain_ref, mid_ref, b_ref, oo_ref, o_s):
    half = o_ref.shape[1]
    for r in range(rows):
        for z in range(parts):
            left = o_ref[r * parts + z].astype(jnp.float32)
            right = o_ref[(rows + r) * parts + z].astype(jnp.float32)
            for n, piece in enumerate(join_pairs(left, right)):
                at = (2 * r + n) * half
                o_s[at : at + half, z * 3 * LN : (z + 1) * 3 * LN] = piece.astype(jnp.bfloat16)
    attended = o_s[...]
    oo_ref[...] = attended
    middle = tok_ref[...].astype(jnp.float32) + dotf(attended, w_ref[...], ((1,), (1,)))
    mid_ref[...] = middle
    factor = lax.rsqrt(jnp.mean(middle * middle, axis=-1, keepdims=True) + EPS)
    b_ref[...] = (middle * factor * gain_ref[...]).astype(jnp.bfloat16)


def out_call(o_parts, weight, tokens, gain, rows):
    count, width = tokens.shape
    inner = weight.shape[1]
    operands = (o_parts, weight, tokens, gain)
    shapes = [
        jax.ShapeDtypeStruct((count, width), jnp.float32),
        jax.ShapeDtypeStruct((count, width), jnp.bfloat16),
        jax.ShapeDtypeStruct((count, inner), jnp.bfloat16),
    ]
    return pl.pallas_call(
        partial(out_kernel, rows, o_parts.shape[0] // (2 * rows)),
        grid=(1,),
        in_specs=[full_spec(v) for v in operands],
        out_specs=[full_spec(v) for v in shapes],
        out_shape=shapes,
        scratch_shapes=[pltpu.VMEM((count, inner), jnp.bfloat16)],
        compiler_params=pltpu.CompilerParams(vmem_limit_bytes=48 << 20),
        name="out_norm",
        cost_estimate=cost(4),
    )(*operands)


def split_pairs(firsts, lasts):
    f0, f1, f2 = thirds(firsts)
    g0, g1, g2 = thirds(lasts)
    low = lane_iota(firsts.shape[0]) < 64
    t0, t1 = pltpu.roll(g0, 64, 1), pltpu.roll(g1, 64, 1)
    left = (f0, jnp.where(low, f1, t0), jnp.where(low, t0, t1))
    u1, u2 = pltpu.roll(f1, 64, 1), pltpu.roll(f2, 64, 1)
    right = (jnp.where(low, u1, u2), jnp.where(low, u2, g1), g2)
    return jnp.concatenate(left, axis=1), jnp.concatenate(right, axis=1)


def mid_back_kernel(
    rows, parts, keep_ref, fx_ref, fy_ref, px_ref, py_ref, mid_ref, cot_ref, gain_ref, w_ref,
    gmid_ref, go_ref, do_ref, gg_ref
):
    half = px_ref.shape[0]
    wide = lambda v: v.astype(jnp.float32)
    db = jnp.concatenate(
        [
            keep_ref[:half] + wide(fx_ref[...]) + wide(py_ref[...]),
            keep_ref[half:] + wide(fy_ref[...]) + wide(px_ref[...]),
        ],
        axis=0,
    )
    middle = mid_ref[...]
    factor = lax.rsqrt(jnp.mean(middle * middle, axis=-1, keepdims=True) + EPS)
    scaled = db * gain_ref[...]
    inner = jnp.mean(scaled * middle, axis=-1, keepdims=True)
    grad = cot_ref[...].astype(jnp.float32) + factor * scaled - middle * (factor**3 * inner)
    gmid_ref[...] = grad
    gg_ref[...] = jnp.sum(db * middle * factor, axis=0, keepdims=True)
    low = grad.astype(jnp.bfloat16)
    go_ref[...] = low
    back = dotf(low, w_ref[...], ((1,), (0,)))
    half = do_ref.shape[1]
    for r in range(rows):
        for z in range(parts):
            cols = slice(z * 3 * LN, (z + 1) * 3 * LN)
            at = 2 * r * half
            left, right = split_pairs(back[at : at + half, cols], back[at + half : at + 2 * half, cols])
            do_ref[r * parts + z] = left.astype(jnp.bfloat16)
            do_ref[(rows + r) * parts + z] = right.astype(jnp.bfloat16)


def mid_back_call(pieces, middle, cot, gain, weight, rows, parts):
    count, width = middle.shape
    operands = (*pieces, middle, cot, gain, weight)
    shapes = [
        jax.ShapeDtypeStruct((count, width), jnp.float32),
        jax.ShapeDtypeStruct((count, width), jnp.bfloat16),
        jax.ShapeDtypeStruct((2 * rows * parts, count // rows // 2, 3 * LN), jnp.bfloat16),
        jax.ShapeDtypeStruct((1, width), jnp.float32),
    ]
    return pl.pallas_call(
        partial(mid_back_kernel, rows, parts),
        grid=(1,),
        in_specs=[pl.BlockSpec((count, width), lambda i: (0, 0))] + [full_spec(v) for v in operands[1:]],
        out_specs=[full_spec(v) for v in shapes],
        out_shape=shapes,
        compiler_params=pltpu.CompilerParams(vmem_limit_bytes=48 << 20),
        name="mid_back",
        cost_estimate=cost(5),
    )(*operands)


def da_kernel(parts, rows, h_ref, d_ref, w_ref, wo_ref, da_ref, gg_ref):
    count = h_ref.shape[0] // parts
    tokens = count // rows
    groups = d_ref.shape[0]
    run = wo_ref.shape[0] // parts
    gg_ref[...] = jnp.zeros_like(gg_ref)

    def body(z, carry):
        at = pl.ds(pl.multiple_of(z * tokens, tokens), tokens)
        left = jnp.concatenate(
            [jnp.concatenate([d_ref[g, r, at, :] for r in range(rows)], axis=0) for g in range(groups)],
            axis=1,
        )
        back = dotf(left, w_ref[...], ((1,), (1,)))
        stream = h_ref[pl.ds(pl.multiple_of(z * count, count), count), :].astype(jnp.float32)
        factor = lax.rsqrt(jnp.mean(stream * stream, axis=-1, keepdims=True) + EPS)
        gg_ref[...] += jnp.sum(back * stream * factor, axis=0, keepdims=True)
        da_ref[z, :count, :] = back.astype(jnp.bfloat16)
        cols = pl.ds(pl.multiple_of(z * 3 * LN, 3 * LN), 3 * LN)
        for n in range(parts):
            da_ref[z, count:, n * 3 * LN : (n + 1) * 3 * LN] = wo_ref[n * run : (n + 1) * run, cols]
        return carry

    lax.fori_loop(0, parts, body, 0)


def da_call(parts, group, grads, weight, grad_wo, rows):
    count, width = group.shape
    operands = (group, grads, weight, grad_wo)
    block = (count + grad_wo.shape[0]) // parts
    shapes = [
        jax.ShapeDtypeStruct((parts, block, width), jnp.bfloat16),
        jax.ShapeDtypeStruct((1, width), jnp.float32),
    ]
    part, gain_grad = pl.pallas_call(
        partial(da_kernel, parts, rows),
        grid=(1,),
        in_specs=[full_spec(v) for v in operands],
        out_specs=[full_spec(v) for v in shapes],
        out_shape=shapes,
        compiler_params=pltpu.CompilerParams(vmem_limit_bytes=48 << 20),
        name="da_part",
        cost_estimate=cost(6),
    )(*operands)
    return part.reshape(parts * block, width), gain_grad


def cut_kernel(gate_ref, up_ref, down_ref, out_ref):
    def body(n, carry):
        at = pl.ds(pl.multiple_of(n * LN, LN), LN)
        out_ref[n, :, :LN] = gate_ref[:, at]
        out_ref[n, :, LN : 2 * LN] = up_ref[:, at]
        out_ref[n, :, 2 * LN :] = jnp.transpose(down_ref[at, :].astype(jnp.float32)).astype(jnp.bfloat16)
        return carry

    lax.fori_loop(0, out_ref.shape[0], body, 0)


def cut_call(gate, up, down):
    shape = jax.ShapeDtypeStruct((gate.shape[1] // LN, gate.shape[0], 3 * LN), jnp.bfloat16)
    operands = (gate, up, down)
    return pl.pallas_call(
        cut_kernel,
        grid=(1,),
        in_specs=[full_spec(v) for v in operands],
        out_specs=full_spec(shape),
        out_shape=shape,
        name="cut_units",
        cost_estimate=cost(3),
    )(*operands)


def uncut_kernel(in_ref, gate_ref, up_ref, down_ref):
    def body(n, carry):
        at = pl.ds(pl.multiple_of(n * LN, LN), LN)
        gate_ref[:, at] = in_ref[n, :, :LN].astype(jnp.float32)
        up_ref[:, at] = in_ref[n, :, LN : 2 * LN].astype(jnp.float32)
        down_ref[at, :] = jnp.transpose(in_ref[n, :, 2 * LN :].astype(jnp.float32))
        return carry

    lax.fori_loop(0, in_ref.shape[0], body, 0)


def uncut_call(value):
    units, rows = value.shape[0] * LN, value.shape[1]
    shapes = [jax.ShapeDtypeStruct(s, jnp.float32) for s in ((rows, units), (rows, units), (units, rows))]
    return pl.pallas_call(
        uncut_kernel,
        grid=(1,),
        in_specs=[full_spec(value)],
        out_specs=[full_spec(v) for v in shapes],
        out_shape=shapes,
        name="uncut_units",
        cost_estimate=cost(3),
    )(value)


def place_kernel(parts, turned, at_ref, mine_ref, other_ref, out_ref):
    size = mine_ref.shape[1]
    z = at_ref[3]
    for c, ref in enumerate((mine_ref, other_ref)):
        for n in range(parts):
            y, x = at_ref[0] ^ (n // 2), at_ref[1] ^ (n % 2)
            rows = pl.multiple_of(((y * 2 + x) * 2 + (at_ref[2] ^ c)) * size, size)
            for k in range(ref.shape[0] // parts):
                count = ref.shape[0] // parts
                source = lax.rem(z + (count - k), count) if turned else k
                cols = pl.multiple_of(source * 3 * LN, 3 * LN)
                out_ref[pl.ds(rows, size), pl.ds(cols, 3 * LN)] = ref[n * count + k]


def place_call(at, mine, other, turned):
    size = mine.shape[1]
    shape = jax.ShapeDtypeStruct((8 * size, mine.shape[0] // 4 * mine.shape[2]), mine.dtype)
    return pl.pallas_call(
        partial(place_kernel, 4, turned),
        grid=(1,),
        in_specs=[pl.BlockSpec(memory_space=pltpu.SMEM), full_spec(mine), full_spec(other)],
        out_specs=full_spec(shape),
        out_shape=shape,
        compiler_params=pltpu.CompilerParams(vmem_limit_bytes=32 << 20),
        name="place_out",
        cost_estimate=cost(3),
    )(at, mine, other)


def fill_sides(refs, out_ref):
    own, xn, yn = refs
    count = own.shape[0]
    half = count // 2
    out_ref[:count] = own[...]
    out_ref[count : count + half], out_ref[count + half : 2 * count] = xn[:half], yn[half:]
    out_ref[2 * count : 2 * count + half], out_ref[2 * count + half : 3 * count] = xn[half:], yn[:half]


def fill_corner(refs, out_ref, at):
    first, last = refs
    half = first.shape[0]
    out_ref[at : at + half], out_ref[at + half : at + 2 * half] = first[...], last[...]


def fill_square(refs, out_ref):
    fill_sides(refs[:3], out_ref)
    fill_corner(refs[3:], out_ref, 3 * refs[0].shape[0])


def unit_spec(weight):
    return pl.BlockSpec((1,) + weight.shape[1:], lambda z: (z, 0, 0))


def row_tiles(rows, tile, body):
    def step(m, carry):
        body(pl.ds(pl.multiple_of(m * tile, tile), tile))
        return carry

    lax.fori_loop(0, rows // tile, step, 0)


def down_back_kernel(*refs):
    pieces, (w0_ref, w1_ref, out_ref, g_s) = refs[:5], refs[5:]

    @pl.when(pl.program_id(0) == 0)
    def _():
        fill_square(pieces, g_s)

    weight = jnp.concatenate([w0_ref[0, :, 2 * LN :], w1_ref[0, :, 2 * LN :]], axis=1)

    def body(at):
        out_ref[0, at] = dotf(g_s[at, :], weight, ((1,), (0,)))

    row_tiles(g_s.shape[0], g_s.shape[0] // 2, body)


def down_back_call(pieces, mine, other):
    count, width = pieces[0].shape
    parts = mine.shape[0]
    shape = jax.ShapeDtypeStruct((parts, 4 * count, 2 * LN), jnp.float32)
    return pl.pallas_call(
        down_back_kernel,
        grid=(parts,),
        in_specs=[full_spec(v) for v in pieces] + [unit_spec(mine), unit_spec(other)],
        out_specs=unit_spec(shape),
        out_shape=shape,
        scratch_shapes=[pltpu.VMEM((4 * count, width), jnp.bfloat16)],
        compiler_params=pltpu.CompilerParams(vmem_limit_bytes=60 << 20),
        name="down_back",
        cost_estimate=cost(8),
    )(*pieces, mine, other)


def units_kernel(count, start, tile, *refs):
    pieces = refs[:2] if start else refs[:3]
    w0_ref, w1_ref, dh_ref, dgu_ref, hid_ref, *sends, b_s, acc_s = refs[len(pieces) :]
    step = pl.program_id(0)

    @pl.when(step == 0)
    def _():
        if start:
            fill_corner(pieces, b_s, 0)
        else:
            fill_sides(pieces, b_s)

    def body(at):
        b = b_s[at, :]
        total = None
        for n, w_ref in enumerate((w0_ref, w1_ref)):
            weight = w_ref[0, :, : 2 * LN]
            both = dotf(b, weight, ((1,), (0,)))
            gate, up = both[:, :LN], both[:, LN:]
            cols = slice(n * LN, (n + 1) * LN)
            dh = dh_ref[0, pl.ds(start + at.start, tile), cols]
            sigma = 1.0 / (1.0 + jnp.exp(-gate))
            silu = gate * sigma
            hid_ref[0, at, cols] = (silu * up).astype(jnp.bfloat16)
            grad_gate = dh * up * sigma * (1.0 + gate * (1.0 - sigma))
            grads = jnp.concatenate([grad_gate, dh * silu], axis=1).astype(jnp.bfloat16)
            dgu_ref[0, n, at] = grads
            back = dotf(grads, weight, ((1,), (1,)))
            total = back if total is None else total + back

        @pl.when(step == 0)
        def _():
            acc_s[at, :] = total

        @pl.when(step > 0)
        def _():
            acc_s[at, :] += total

    row_tiles(b_s.shape[0], tile, body)

    @pl.when(step == pl.num_programs(0) - 1)
    def _():
        half = count // 2
        if start:
            sx_ref, sy_ref = sends
            sx_ref[...] = acc_s[:half].astype(jnp.bfloat16)
            sy_ref[...] = acc_s[half:].astype(jnp.bfloat16)
        else:
            keep_ref, sx_ref, sy_ref = sends
            keep_ref[:count] = acc_s[:count]
            keep_ref[count:] = acc_s[2 * count :]
            sx_ref[...] = acc_s[count : count + half].astype(jnp.bfloat16)
            sy_ref[...] = acc_s[count + half : 2 * count].astype(jnp.bfloat16)


def units_call(pieces, mine, other, grad_hidden, corner):
    parts, width = mine.shape[:2]
    count = grad_hidden.shape[1] // 4
    rows = count if corner else 3 * count
    low = jnp.bfloat16
    shapes = [
        jax.ShapeDtypeStruct((parts, 2, rows, 2 * LN), low),
        jax.ShapeDtypeStruct((parts, rows, 2 * LN), low),
    ]
    if not corner:
        shapes += [jax.ShapeDtypeStruct((2 * count, width), jnp.float32)]
    shapes += [jax.ShapeDtypeStruct((count // 2, width), low)] * 2
    return pl.pallas_call(
        partial(units_kernel, count, 3 * count if corner else 0, count),
        grid=(parts,),
        in_specs=[full_spec(v) for v in pieces] + [unit_spec(mine), unit_spec(other), unit_spec(grad_hidden)],
        out_specs=[
            pl.BlockSpec((1, 2, rows, 2 * LN), lambda z: (z, 0, 0, 0)),
            pl.BlockSpec((1, rows, 2 * LN), lambda z: (z, 0, 0)),
        ]
        + [full_spec(v) for v in shapes[2:]],
        out_shape=shapes,
        scratch_shapes=[pltpu.VMEM((rows, width), low), pltpu.VMEM((rows, width), jnp.float32)],
        compiler_params=pltpu.CompilerParams(vmem_limit_bytes=60 << 20),
        name="units_corner" if corner else "units",
        cost_estimate=cost(8 if corner else 19),
    )(*pieces, mine, other, grad_hidden)


def down_kernel(hid_ref, hid_last_ref, w0_ref, w1_ref, keep_ref, sx_ref, sy_ref, acc_s):
    step = pl.program_id(0)
    weight = jnp.concatenate([w0_ref[0, :, 2 * LN :], w1_ref[0, :, 2 * LN :]], axis=1)
    rows, count = hid_ref.shape[1], hid_last_ref.shape[1]

    def add(at, hidden):
        total = dotf(hidden, weight, ((1,), (1,)))

        @pl.when(step == 0)
        def _():
            acc_s[at, :] = total

        @pl.when(step > 0)
        def _():
            acc_s[at, :] += total

    row_tiles(rows, count, lambda at: add(at, hid_ref[0, at]))
    add(pl.ds(rows, count), hid_last_ref[0])

    @pl.when(step == pl.num_programs(0) - 1)
    def _():
        half = count // 2
        keep_ref[:count] = acc_s[:count]
        keep_ref[count:] = acc_s[2 * count : 3 * count]
        for n, ref in enumerate((sx_ref, sy_ref)):
            at = n * half
            ref[:half] = acc_s[count + at : count + at + half].astype(jnp.bfloat16)
            ref[half:] = acc_s[3 * count + at : 3 * count + at + half].astype(jnp.bfloat16)


def down_call(hidden, hidden_last, mine, other):
    parts, count, _ = hidden_last.shape
    width = mine.shape[1]
    shapes = [
        jax.ShapeDtypeStruct((2 * count, width), jnp.float32),
        jax.ShapeDtypeStruct((count, width), jnp.bfloat16),
        jax.ShapeDtypeStruct((count, width), jnp.bfloat16),
    ]
    operands = (hidden, hidden_last, mine, other)
    return pl.pallas_call(
        down_kernel,
        grid=(parts,),
        in_specs=[unit_spec(v) for v in operands],
        out_specs=[full_spec(v) for v in shapes],
        out_shape=shapes,
        scratch_shapes=[pltpu.VMEM((4 * count, width), jnp.float32)],
        compiler_params=pltpu.CompilerParams(vmem_limit_bytes=60 << 20),
        name="down",
        cost_estimate=cost(11),
    )(*operands)


def unit_grads_kernel(*refs):
    b_pieces, g_pieces = refs[:5], refs[5:10]
    dgu_ref, dgu_last_ref, hid_ref, hid_last_ref, mine_ref, other_ref, fill_s, b_s, g_s = refs[10:]
    total, width = fill_s.shape
    count = total // 4

    @pl.when(pl.program_id(0) == 0)
    def _():
        for pieces, side in ((b_pieces, b_s), (g_pieces, g_s)):
            fill_square(pieces, fill_s)
            for m in range(4):
                at = slice(m * count, (m + 1) * count)
                side[:, at] = jnp.transpose(fill_s[at, :])

    cut = hid_ref.shape[1]

    def body(at):
        left, right = b_s[at, :], g_s[at, :]
        sum_over = lambda v, a, z: dotf(v[:, :cut], a, ((1,), (0,))) + dotf(v[:, cut:], z, ((1,), (0,)))
        down = sum_over(right, hid_ref[0], hid_last_ref[0])
        for n, out_ref in enumerate((mine_ref, other_ref)):
            out_ref[0, at, : 2 * LN] = sum_over(left, dgu_ref[0, n], dgu_last_ref[0, n]).astype(jnp.bfloat16)
            out_ref[0, at, 2 * LN :] = down[:, n * LN : (n + 1) * LN].astype(jnp.bfloat16)

    row_tiles(width, width // 4, body)


def unit_grads_call(b_pieces, g_pieces, grads, hidden):
    count, width = b_pieces[0].shape
    parts = hidden[0].shape[0]
    low = jnp.bfloat16
    operands = (*b_pieces, *g_pieces)
    return pl.pallas_call(
        unit_grads_kernel,
        grid=(parts,),
        in_specs=[full_spec(v) for v in operands]
        + [pl.BlockSpec((1,) + v.shape[1:], lambda z: (z, 0, 0, 0)) for v in grads]
        + [unit_spec(v) for v in hidden],
        out_specs=[pl.BlockSpec((1, width, 3 * LN), lambda z: (z, 0, 0))] * 2,
        out_shape=[jax.ShapeDtypeStruct((parts, width, 3 * LN), low)] * 2,
        scratch_shapes=[pltpu.VMEM((4 * count, width), low)] + [pltpu.VMEM((width, 4 * count), low)] * 2,
        compiler_params=pltpu.CompilerParams(vmem_limit_bytes=60 << 20),
        name="unit_grads",
        cost_estimate=cost(19),
    )(*operands, *grads, *hidden)


BY_SIDES = tuple((y, x, last) for x in range(2) for y in range(2) for last in range(2))
ORDER = ((0, 0, 0), (0, 0, 1), (0, 1, 0), (1, 1, 0), (1, 0, 1), (1, 1, 1), (0, 1, 1), (1, 0, 0))


def row_grads_kernel(order, at_ref, left_ref, right_ref, mine_ref, other_ref, full_s):
    tile = 2 * LN
    width = right_ref.shape[2]

    def body(n, carry):
        rows = pl.ds(pl.multiple_of(n * tile, tile), tile)
        left = jnp.transpose(left_ref[:, rows])
        for g in range(right_ref.shape[0]):
            piece = dotf(left, right_ref[g], ((1,), (0,)))
            full_s[rows, g * width : (g + 1) * width] = piece.astype(jnp.bfloat16)
        return carry

    lax.fori_loop(0, full_s.shape[0] // tile, body, 0)
    half = mine_ref.shape[1]
    for c, out_ref in enumerate((mine_ref, other_ref)):
        for n, (y, x, last) in enumerate(order):
            block = ((at_ref[0] ^ y) * 2 + (at_ref[1] ^ x)) * 2 + (at_ref[2] ^ c)
            rows = pl.multiple_of(block * 2 * half + last * half, 32)
            out_ref[n] = full_s[pl.ds(rows, half), :]


def row_grads_call(at, left, right, order, name, time):
    width = left.shape[1]
    cols = right.shape[0] * right.shape[2]
    shape = jax.ShapeDtypeStruct((8, width // 16, cols), jnp.bfloat16)
    return pl.pallas_call(
        partial(row_grads_kernel, order),
        grid=(1,),
        in_specs=[pl.BlockSpec(memory_space=pltpu.SMEM), full_spec(left), full_spec(right)],
        out_specs=[full_spec(shape)] * 2,
        out_shape=[shape] * 2,
        scratch_shapes=[pltpu.VMEM((width, cols), jnp.bfloat16)],
        compiler_params=pltpu.CompilerParams(vmem_limit_bytes=32 << 20),
        cost_estimate=cost(time),
        name=name,
    )(at, left, right)


def core_sum(mine, other):
    step = mine.shape[1]
    both = (mine.astype(jnp.float32) + other.astype(jnp.float32)).reshape(8 * step, -1)
    keep = jnp.concatenate([both[: 2 * step], both[6 * step :]], axis=0)
    low = both[2 * step : 6 * step].astype(jnp.bfloat16)
    return keep, low[: 2 * step], low[2 * step :]


EVERY = ("y", "x", "c", "z")
SWAP = ((0, 1), (1, 0))


def swap(value, axis):
    return lax.ppermute(value, axis, SWAP)


def gather_blocks(value, size):
    shift = lambda k: [(i, (i + k) % size) for i in range(size)]
    return [value] + [lax.ppermute(value, "z", shift(k)) for k in range(1, size)]


def gather_sides(value):
    return swap(value, "x"), swap(value, "y")


def gather_corner(xn, yn):
    half = xn.shape[0] // 2
    return swap(yn[:half], "x"), swap(xn[half:], "y")


def gather_square(value):
    sides = gather_sides(value)
    return (value, *sides, *gather_corner(*sides))


def reduce_square(keep, send_x, send_y):
    return reduce_square_rest(keep, swap(send_x, "x"), swap(send_y, "y"))


def reduce_square_rest(keep, from_x, from_y):
    half = from_x.shape[0] // 2
    corner = pass_on(keep, from_x[half:], from_y[half:])
    return keep, from_x[:half], from_y[:half], *corner


def pass_on(keep, corner_x, corner_y):
    low = jnp.bfloat16
    half = corner_x.shape[0]
    pass_y = swap((keep[3 * half :] + corner_x.astype(jnp.float32)).astype(low), "y")
    pass_x = swap((keep[2 * half : 3 * half] + corner_y.astype(jnp.float32)).astype(low), "x")
    return pass_x, pass_y


def total_square(pieces):
    keep, from_x, from_y, pass_x, pass_y = pieces
    half = pass_x.shape[0]
    wide = lambda v: v.astype(jnp.float32)
    return jnp.concatenate(
        [
            keep[:half] + wide(from_x) + wide(pass_y),
            keep[half : 2 * half] + wide(from_y) + wide(pass_x),
        ],
        axis=0,
    )


def all_to_all(value, axes):
    return lax.all_to_all(value, axes, 0, 0, tiled=True)


def tie(*values):
    return lax.optimization_barrier(values)


def fast_local(sizes, *args):
    (tokens, cotangent, segments, positions, norm_in, w_query, w_key, w_value, w_out, norm_mid, w_gate, w_up, w_down) = args
    nz = sizes["z"]
    devices = sizes["y"] * sizes["x"] * sizes["c"] * nz
    plane = devices // nz
    rows, span, width = tokens.shape
    count = rows * span
    chunk = segments.shape[1]
    length = chunk * sizes["x"] * sizes["c"]
    x_at, c_at, z_at = lax.axis_index("x"), lax.axis_index("c"), lax.axis_index("z")
    at = jnp.stack([lax.axis_index("y"), x_at, c_at, z_at]).astype(jnp.int32)

    own = tokens.reshape(count, width)
    group = lax.all_gather(own, "z", axis=0, tiled=True)
    gains = jnp.concatenate([norm_in, norm_mid], axis=1)
    share = norm_in.shape[1]
    gains = jnp.pad(gains, ((0, 0), (0, LN - 2 * share)))
    gains = all_to_all(jnp.broadcast_to(gains, (devices, LN)), EVERY)

    kv_local = w_key.shape[2] // HD
    per_head = lambda w: w[0].reshape(w.shape[1], kv_local, -1)
    w_qkv = jnp.concatenate([per_head(w_query), per_head(w_key), per_head(w_value)], axis=2)
    w_qkv, w_o = tie(jnp.transpose(w_qkv, (1, 0, 2)), jnp.stack(gather_blocks(w_out[0].T, nz)))
    w_qkv = jnp.concatenate(gather_square(w_qkv), axis=0)
    w_qkv = place_call(at, w_qkv, swap(w_qkv, "c"), False)

    last = (x_at * sizes["c"] + c_at + 1) * chunk - 1
    begin = last - positions[:, -1] - jnp.where(segments[:, -1] == 2, 3 * length // 4, 0)
    lanes = jnp.arange(LN, dtype=jnp.int32) % (HD // 2)
    frequency = THETA ** (-(2.0 * lanes.astype(jnp.float32)) / HD)
    token_angle = positions.astype(jnp.float32)[:, :, None] * frequency
    first = lax.dynamic_slice_in_dim(begin, c_at, 1).astype(jnp.int32)
    index = jnp.arange(length, dtype=jnp.int32)
    row_angle = (index - doc_low(index, first[0], length)).astype(jnp.float32)[:, None] * frequency
    token_cos, token_sin = jnp.cos(token_angle), jnp.sin(token_angle)
    row_cos, row_sin = jnp.cos(row_angle), jnp.sin(row_angle)

    sides = gather_sides(w_o)
    gate, up, down, gains, *tables = tie(
        w_gate[0], w_up[0], w_down[0], gains, token_cos, token_sin, row_cos, row_sin, *sides
    )
    token_cos, token_sin, row_cos, row_sin, *sides = tables
    gain_in = gains[:, :share].reshape(1, width)
    gain_mid = gains[:, share : 2 * share].reshape(1, width)
    w_ff = all_to_all(cut_call(gate, up, down), ("y", "x", "c"))
    w_ff = w_ff.reshape(width, 3 * LN)
    corner = gather_corner(*sides)
    group, w_qkv, w_ff = tie(group, w_qkv, w_ff)
    w_mine = lax.all_gather(w_ff, "z", axis=0, tiled=True)

    normed, qkv = qkv_call(nz, group, gain_in, w_qkv, token_cos, token_sin, rows)
    qkv, *corner = tie(qkv, *corner)
    w_o = jnp.concatenate([w_o, *sides, *corner], axis=0)
    qkv = all_to_all(qkv, ("x", "c")).reshape(length, 3 * LN)

    cot_low = cotangent.reshape(count, width)
    cot_first, _ = tie(cot_low, qkv)
    cot_sides = gather_sides(cot_first)

    attended, attended_float, log_total = attn_fwd(first, qkv)
    attended, *cot_sides = tie(attended, *cot_sides)
    attended = all_to_all(attended, ("x", "c", "z"))
    w_o = place_call(at, w_o, swap(w_o, "c"), True)
    w_o, *cot_sides = tie(w_o, *cot_sides)
    attended, *corner = tie(attended, *gather_corner(*cot_sides))
    cot_pieces = (cot_low, *cot_sides, *corner)
    middle, normed_b, attended_low = out_call(attended, w_o, own, gain_mid, rows)
    w_mine, _ = tie(w_mine, normed_b)
    w_mine = w_mine.reshape(nz, width, 3 * LN)
    w_other = swap(w_mine, "c")
    b_sides = gather_sides(normed_b)
    grad_hidden = down_back_call(cot_pieces, w_mine, w_other)
    *b_sides, grad_hidden = tie(*b_sides, grad_hidden)
    b_corner = gather_corner(*b_sides)
    b_pieces = (normed_b, *b_sides, *b_corner)
    grads, hidden, keep_b, *sends = units_call((normed_b, *b_sides), w_mine, w_other, grad_hidden, False)
    from_x, from_y = swap(sends[0], "x"), swap(sends[1], "y")
    grads_last, hidden_last, *sends = units_call(b_corner, w_mine, w_other, grad_hidden, True)
    corner_x, corner_y = swap(sends[0], "x"), swap(sends[1], "y")
    ff_mine, ff_other = unit_grads_call(b_pieces, cot_pieces, (grads, grads_last), (hidden, hidden_last))
    from_x, from_y, corner_x, corner_y, ff_other = tie(from_x, from_y, corner_x, corner_y, ff_other)
    grad_b = (keep_b, from_x, from_y, *pass_on(keep_b, corner_x, corner_y))
    grad_ff = ff_mine.astype(jnp.float32) + swap(ff_other, "c").astype(jnp.float32)
    grad_ff = grad_ff.astype(jnp.bfloat16).reshape(nz * width, 3 * LN)
    grad_ff, *corner = tie(grad_ff, *grad_b[3:])
    grad_b = (*grad_b[:3], *corner)
    grad_ff = lax.psum_scatter(grad_ff, "z", scatter_dimension=0, tiled=True)
    grad_mid, grad_low, grad_o, gain_grad_mid = mid_back_call(
        grad_b, middle, cot_low, gain_mid, w_o, rows, nz
    )
    grad_o = all_to_all(grad_o, ("x", "c", "z"))
    hidden, hidden_last, _ = tie(hidden, hidden_last, grad_low)
    keep_out, *out_sides = down_call(hidden, hidden_last, w_mine, w_other)
    out_sides = swap(out_sides[0], "x"), swap(out_sides[1], "y")
    wo_mine, wo_other = row_grads_call(at, grad_low, attended_low[None], BY_SIDES, "out_grads", 3)
    wo_sum = (wo_mine.astype(jnp.float32) + swap(wo_other, "c").astype(jnp.float32)).reshape(width // 2, -1)
    wo_keep, wo_send = wo_sum[: width // 4], wo_sum[width // 4 :].astype(jnp.bfloat16)
    wo_got = swap(wo_send, "x")

    grad_qkv = attn_bwd(first, qkv, grad_o, attended_float, log_total, row_cos, row_sin)
    grad_qkv, wo_got, *out_sides = tie(grad_qkv, wo_got, *out_sides)
    out = middle + total_square(reduce_square_rest(keep_out, *out_sides))
    wo_sum = wo_keep + wo_got.astype(jnp.float32)
    wo_got = swap(wo_sum[width // 8 :].astype(jnp.bfloat16), "y")
    grad_wo = (wo_sum[: width // 8] + wo_got.astype(jnp.float32)).astype(jnp.bfloat16)
    grad_qkv = all_to_all(grad_qkv.reshape(-1, chunk, 3 * LN), ("x", "c"))
    grad_qkv, grad_ff = tie(grad_qkv, grad_ff)
    grad_ff = all_to_all(grad_ff.reshape(plane, width // plane, 3 * LN), ("y", "x", "c"))
    grad_qkv = grad_qkv.reshape(kv_local, rows, chunk, 3 * LN)
    part, gain_grad_in = da_call(nz, group, grad_qkv, w_qkv, grad_wo, rows)
    part = lax.psum_scatter(part, "z", scatter_dimension=0, tiled=True).astype(jnp.float32)
    grad_a, grad_wo = part[:count], part[count:]
    grad_wo = jnp.concatenate([grad_wo[:, n * 3 * LN : (n + 1) * 3 * LN] for n in range(nz)], axis=0)
    grad_wqkv = row_grads_call(
        at,
        normed.reshape(rows * chunk, width),
        grad_qkv.reshape(kv_local, rows * chunk, 3 * LN),
        ORDER,
        "qkv_grads",
        5,
    )
    *grad_wqkv, grad_ff = tie(*grad_wqkv, grad_ff)
    grad_wqkv = reduce_square(*core_sum(grad_wqkv[0], swap(grad_wqkv[1], "c")))
    gain_grads = jnp.concatenate(
        [gain_grad_in.reshape(devices, share), gain_grad_mid.reshape(devices, share)], axis=1
    )
    gain_grads = jnp.pad(gain_grads, ((0, 0), (0, LN - 2 * share)))
    *grad_wqkv, gain_grads = tie(*grad_wqkv, gain_grads)
    grad_wqkv = total_square(grad_wqkv)
    gain_grads = jnp.sum(all_to_all(gain_grads, EVERY), axis=0, keepdims=True)

    stream = own.astype(jnp.float32)
    factor = lax.rsqrt(jnp.mean(stream * stream, axis=-1, keepdims=True) + EPS)
    back_in, _ = norm_back(stream, factor, gain_in, grad_a)
    grad_tokens = grad_mid + back_in
    grad_wqkv = grad_wqkv.reshape(-1, kv_local, 4 * HD)
    flat = lambda g: g.reshape(1, g.shape[0], -1)
    grad_gate, grad_up, grad_down = uncut_call(grad_ff)
    return (
        out.reshape(tokens.shape),
        grad_tokens.reshape(tokens.shape),
        gain_grads[:, :share],
        flat(grad_wqkv[:, :, : 2 * HD]),
        flat(grad_wqkv[:, :, 2 * HD : 3 * HD]),
        flat(grad_wqkv[:, :, 3 * HD :]),
        grad_wo.T[None],
        gain_grads[:, share : 2 * share],
        grad_gate[None],
        grad_up[None],
        grad_down[None],
    )


def fast_solution(mesh, cores):
    batch, seq, kv = mesh.devices.shape
    fine = Mesh(mesh.devices.reshape(batch, seq // cores, cores, kv), EVERY)
    sizes = dict(fine.shape)
    row_spec = P("y", ("x", "c", "z"), None)
    seq_spec = P("y", ("x", "c"))
    gain_spec = P(None, EVERY)
    in_w = P(None, ("y", "x", "c"), "z")
    out_w = P(None, "z", ("y", "x", "c"))
    in_specs = (row_spec, row_spec, seq_spec, seq_spec, gain_spec, in_w, in_w, in_w, out_w, gain_spec, in_w, in_w, out_w)
    out_specs = (row_spec, row_spec, gain_spec, in_w, in_w, in_w, out_w, gain_spec, in_w, in_w, out_w)
    return jax.shard_map(
        partial(fast_local, sizes), mesh=fine, in_specs=in_specs, out_specs=out_specs, check_vma=False
    )


def solution(mesh):
    batch, seq, kv = (mesh.shape[name] for name in ("batch", "seq", "kv"))
    general = general_solution(mesh)
    if (batch, seq) != (2, 4):
        return general
    fast = fast_solution(mesh, 2)

    def run(*args):
        rows, length, width = args[0].shape
        kv_heads, q_heads = args[6].shape[2] // HD, args[5].shape[2] // HD
        fits = (
            rows == 2 * batch
            and kv_heads == 2 * kv
            and q_heads == 2 * kv_heads
            and length == 128 * seq * kv
            and length % (4 * BQ) == 0
            and width % LN == 0
            and 2 * width // (batch * seq * kv) <= LN
            and args[10].shape[2] == LN * batch * seq * kv
        )
        return (fast if fits else general)(*args)

    return run
```

profile of v0, /device:TPU:0, one launch (start us, length us, event | category | flops | bytes accessed | tf_op | source)
XLA Modules:
  0.0 495.8 jit_solution(7563099719385809314)
XLA Ops:
  7.9 4.1 collective-permute-start.1
  13.6 2.2 collective-permute-start.2
  17.2 2.8 all-to-all-start
  29.1 5.6 %multiply_sine_fusion = (f32[2048,128]{1,0:T(8,128)}, f32[2048,128]{1,0:T(8,128)}) fusion(f32[128]{0:T(128)S(1)} %fusion.15, f32[2048]{0:T(1024)S(1)} %subtract_convert_fusion), kind=kLoop, calls=%fused_computation.14 | loop fusion | flops 262144 | bytes 2105856 | tf_op jit(solution)/shard_map/sin | solution.py:1500
  39.1 13.6 %collective-permute-done.5 = bf16[1,192,384]{2,1,0:T(8,128)(2,1)S(1)} collective-permute-done((bf16[1,192,384]{2,1,0:T(8,128)(2,1)S(1)}, bf16[1,192,384]{2,1,0:T(8,128)(2,1)S(1)}, u32[]{:S(2)}, u32[]{:S(2)}) %collective-permute-start.5) | collective-permute-done | bytes 147488 | tf_op jit(solution)/shard_map/ppermute | solution.py:1404
  56.7 3.4 cut_units.1
  60.1 4.3 all-to-all-start.1
  67.4 13.8 %all-to-all-done.1 = bf16[8,192,384]{2,1,0:T(8,128)(2,1)} async-done(((bf16[8,192,384]{2,1,0:T(8,128)(2,1)}), bf16[8,192,384]{2,1,0:T(8,128)(2,1)}, u32[]{:S(2)}, u32[]{:S(2)}) %all-to-all-start.1) | async-done | bytes 1179680 | tf_op jit(solution)/shard_map/all_to_all | solution.py:1458
  86.3 9.0 %norm_qkv.1 = (bf16[2,512,1536]{2,1,0:T(8,128)(2,1)}, bf16[4,512,384]{2,1,0:T(8,128)(2,1)}) custom-call(bf16[1024,1536]{1,0:T(8,128)(2,1)} %all-gather.3.cloned.1.call-done.h_ref, f32[1,1536]{1,0:T(1,128)S(1)} %reshape.188.gain_ref, bf16[1536,768]{1,0:T(8,128)(2,1)S(1)} %copy-done.20, f32[2,512,128]{2,1,0:T(8,128)S(1)} %get-tuple-element.111.cos_ref, ...), custom_call_target="tpu_custom_call" | custom-call | flops 7000000000 | bytes 21000000 | tf_op jit(solution)/shard_map/norm_qkv/pallas_call | solution.py:839
  95.2 3.6 all-to-all-start.2
  104.6 14.3 %all-to-all-done.2 = bf16[4,512,384]{2,1,0:T(8,128)(2,1)S(1)} async-done(((bf16[4,512,384]{2,1,0:T(8,128)(2,1)}), bf16[4,512,384]{2,1,0:T(8,128)(2,1)S(1)}, u32[]{:S(2)}, u32[]{:S(2)}) %all-to-all-start.2) | async-done | bytes 1572896 | tf_op jit(solution)/shard_map/all_to_all | solution.py:1458
  120.7 18.2 %attend.1 = (bf16[16,64,384]{2,1,0:T(8,128)(2,1)}, f32[8,512,128]{2,1,0:T(8,128)S(1)}, f32[8,8,512]{2,1,0:T(8,128)S(1)}) custom-call(s32[1]{0:T(128)} %bitcast.first_ref, bf16[2048,384]{1,0:T(8,128)(2,1)S(1)} %bitcast.75), custom_call_target="tpu_custom_call" | custom-call | flops 22000001024 | bytes 66000000 | tf_op jit(solution)/shard_map/attend/pallas_call | solution.py:647
  142.7 14.6 %all-to-all-start.3 = ((bf16[16,64,384]{2,1,0:T(8,128)(2,1)}), bf16[16,64,384]{2,1,0:T(8,128)(2,1)S(1)}, u32[]{:S(2)}, u32[]{:S(2)}) async-start(bf16[16,64,384]{2,1,0:T(8,128)(2,1)} %get-tuple-element.119), calls=%async_computation.3 | async-start | bytes 1572864 | tf_op jit(solution)/shard_map/all_to_all | solution.py:1458
  157.4 2.9 place_out.3.w_ref
  160.3 2.2 copy-done.18
  165.3 8.8 %collective-permute-done.16.refs_4_.refs_9_ = bf16[128,1536]{1,0:T(8,128)(2,1)S(1)} collective-permute-done((bf16[128,1536]{1,0:T(8,128)(2,1)S(1)}, bf16[128,1536]{1,0:T(8,128)(2,1)S(1)}, u32[]{:S(2)}, u32[]{:S(2)}) %collective-permute-start.16) | collective-permute-done | bytes 393248 | tf_op jit(solution)/shard_map/ppermute | solution.py:1404
  174.0 3.9 collective-permute-done.15.refs_3_.refs_8_
  177.9 17.0 %all-to-all-done.3.o_ref = bf16[16,64,384]{2,1,0:T(8,128)(2,1)S(1)} async-done(((bf16[16,64,384]{2,1,0:T(8,128)(2,1)}), bf16[16,64,384]{2,1,0:T(8,128)(2,1)S(1)}, u32[]{:S(2)}, u32[]{:S(2)}) %all-to-all-start.3) | async-done | bytes 786464 | tf_op jit(solution)/shard_map/all_to_all | solution.py:1458
  195.0 4.0 out_norm.1
  203.3 6.0 %collective-permute-done.19.refs_6_.refs_4_.refs_3_.w1_ref = bf16[4,1536,384]{2,1,0:T(8,128)(2,1)} collective-permute-done((bf16[4,1536,384]{2,1,0:T(8,128)(2,1)}, bf16[4,1536,384]{2,1,0:T(8,128)(2,1)}, u32[]{:S(2)}, u32[]{:S(2)}) %collective-permute-start.19) | collective-permute-done | bytes 4718624 | tf_op jit(solution)/shard_map/ppermute | solution.py:1404
  209.3 9.6 %down_back.1.refs_5_.refs_4_ = f32[4,1024,256]{2,1,0:T(8,128)} custom-call(bf16[256,1536]{1,0:T(8,128)(2,1)} %bitcast.79, bf16[256,1536]{1,0:T(8,128)(2,1)} %copy-done.32, bf16[256,1536]{1,0:T(8,128)(2,1)} %copy-done.30, bf16[128,1536]{1,0:T(8,128)(2,1)} %copy-done.45, bf16[128,1536]{1,0:T(8,128)(2,1)} %copy-done.44, bf16[4,1536,384]{2,1,0:T(8,128)(2,1)} %bitcast.108, ...), custom_call_target="tpu_custom_call" | custom-call | flops 8000000000 | bytes 24000000 | tf_op jit(solution)/shard_map/down_back/pallas_call | solution.py:1153
  218.9 2.1 collective-permute-done.18.refs_2_
  224.6 21.3 %units.1 = (bf16[4,2,768,256]{3,2,1,0:T(8,128)(2,1)}, bf16[4,768,256]{2,1,0:T(8,128)(2,1)}, f32[512,1536]{1,0:T(8,128)}, bf16[128,1536]{1,0:T(8,128)(2,1)}, bf16[128,1536]{1,0:T(8,128)(2,1)}) custom-call(bf16[256,1536]{1,0:T(8,128)(2,1)} %copy-done.12, bf16[256,1536]{1,0:T(8,128)(2,1)} %collective-permute-done.17.refs_1_, bf16[256,1536]{1,0:T(8,128)(2,1)} %copy-done.34, ...), custom_call_target="tpu_custom_call" | custom-call | flops 19000000512 | bytes 57000000 | tf_op jit(solution)/shard_map/units/pallas_call | solution.py:1233
  249.6 9.8 %units_corner.1 = (bf16[4,2,256,256]{3,2,1,0:T(8,128)(2,1)}, bf16[4,256,256]{2,1,0:T(8,128)(2,1)}, bf16[128,1536]{1,0:T(8,128)(2,1)}, bf16[128,1536]{1,0:T(8,128)(2,1)}) custom-call(bf16[128,1536]{1,0:T(8,128)(2,1)} %copy-done.46, bf16[128,1536]{1,0:T(8,128)(2,1)} %collective-permute-done.21.refs_1_.refs_4_, bf16[4,1536,384]{2,1,0:T(8,128)(2,1)} %bitcast.110, ...), custom_call_target="tpu_custom_call" | custom-call | flops 8000000000 | bytes 24000000 | tf_op jit(solution)/shard_map/units_corner/pallas_call | solution.py:1233
  260.6 19.2 %unit_grads.1 = (bf16[4,1536,384]{2,1,0:T(8,128)(2,1)}, bf16[4,1536,384]{2,1,0:T(8,128)(2,1)}) custom-call(bf16[256,1536]{1,0:T(8,128)(2,1)} %copy-done.12, bf16[256,1536]{1,0:T(8,128)(2,1)} %collective-permute-done.17.refs_1_, bf16[256,1536]{1,0:T(8,128)(2,1)} %copy-done.34, bf16[128,1536]{1,0:T(8,128)(2,1)} %copy-done.46, ...), custom_call_target="tpu_custom_call" | custom-call | flops 19000000512 | bytes 57000000 | tf_op jit(solution)/shard_map/unit_grads/pallas_call | solution.py:1334
  284.5 3.5 collective-permute-done.26
  288.0 5.6 %add_convert_fusion = bf16[4,1536,384]{2,1,0:T(8,128)(2,1)} fusion(bf16[4,1536,384]{2,1,0:T(8,128)(2,1)S(1)} %collective-permute-done.26, bf16[4,1536,384]{2,1,0:T(8,128)(2,1)} %get-tuple-element.149), kind=kLoop, calls=%fused_computation | loop fusion | flops 9437184 | bytes 14155776 | tf_op jit(solution)/shard_map/convert_element_type | solution.py:1548
  297.2 6.4 %mid_back.1 = (f32[256,1536]{1,0:T(8,128)S(1)}, bf16[256,1536]{1,0:T(8,128)(2,1)S(1)}, bf16[16,64,384]{2,1,0:T(8,128)(2,1)S(1)}, f32[1,1536]{1,0:T(1,128)S(1)}) custom-call(f32[512,1536]{1,0:T(8,128)} %get-tuple-element.139.keep_ref, bf16[128,1536]{1,0:T(8,128)(2,1)S(1)} %collective-permute-done.22.fx_ref, ...), custom_call_target="tpu_custom_call" | custom-call | flops 5000000000 | bytes 15000000 | tf_op jit(solution)/shard_map/mid_back/pallas_call | solution.py:964
  304.5 4.6 out_grads.1
  309.2 4.5 all-to-all-start.4
  313.7 13.2 %down.1 = (f32[512,1536]{1,0:T(8,128)}, bf16[256,1536]{1,0:T(8,128)(2,1)}, bf16[256,1536]{1,0:T(8,128)(2,1)}) custom-call(bf16[4,768,256]{2,1,0:T(8,128)(2,1)} %get-tuple-element.156.refs_12_.hid_ref, bf16[4,256,256]{2,1,0:T(8,128)(2,1)} %get-tuple-element.157.refs_13_.hid_last_ref, bf16[4,1536,384]{2,1,0:T(8,128)(2,1)} %bitcast.111, ...), custom_call_target="tpu_custom_call" | custom-call | flops 11000000512 | bytes 33000000 | tf_op jit(solution)/shard_map/down/pallas_call | solution.py:1289
  329.2 2.3 convert_add_fusion
  331.5 2.2 copy-done.24
  334.4 20.1 %all-to-all-done.4.do_ref = bf16[16,64,384]{2,1,0:T(8,128)(2,1)} async-done(((bf16[16,64,384]{2,1,0:T(8,128)(2,1)}), bf16[16,64,384]{2,1,0:T(8,128)(2,1)}, u32[]{:S(2)}, u32[]{:S(2)}) %all-to-all-start.4) | async-done | bytes 786464 | tf_op jit(solution)/shard_map/all_to_all | solution.py:1458
  354.4 27.4 %attend_back.1 = bf16[2048,384]{1,0:T(8,128)(2,1)} custom-call(s32[1]{0:T(128)} %bitcast.first_ref, bf16[2048,384]{1,0:T(8,128)(2,1)} %bitcast.76, bf16[16,64,384]{2,1,0:T(8,128)(2,1)} %all-to-all-done.4.do_ref, f32[8,512,128]{2,1,0:T(8,128)} %copy-done.22, f32[8,8,512]{2,1,0:T(8,128)} %copy-done.23, f32[2048,128]{1,0:T(8,128)} %get-tuple-element.162.cos_ref, ...), custom_call_target="tpu_custom_call" | custom-call | flops 31000000512 | bytes 93000000 | tf_op jit(solution)/shard_map/attend_back/pallas_call | solution.py:754
  383.4 3.6 all-to-all-start.5
  390.6 14.2 %collective-permute-done.35 = bf16[192,1536]{1,0:T(8,128)(2,1)S(1)} collective-permute-done((bf16[192,1536]{1,0:T(8,128)(2,1)S(1)}, bf16[192,1536]{1,0:T(8,128)(2,1)S(1)}, u32[]{:S(2)}, u32[]{:S(2)}) %collective-permute-start.35) | collective-permute-done | bytes 589856 | tf_op jit(solution)/shard_map/ppermute | solution.py:1404
  408.7 7.1 %da_part.1 = (bf16[4,304,1536]{2,1,0:T(8,128)(2,1)}, f32[1,1536]{1,0:T(1,128)S(1)}) custom-call(bf16[1024,1536]{1,0:T(8,128)(2,1)} %all-gather.3.cloned.1.call-done.h_ref, bf16[2,2,512,384]{3,2,1,0:T(8,128)(2,1)S(1)} %bitcast.77, bf16[1536,768]{1,0:T(8,128)(2,1)S(1)} %copy-done.21, bf16[192,1536]{1,0:T(8,128)(2,1)S(1)} %fusion.4.wo_ref), custom_call_target="tpu_custom_call" | custom-call | flops 6000000000 | bytes 18000000 | tf_op jit(solution)/shard_map/da_part/pallas_call | solution.py:1010
  418.9 4.3 all-to-all-start.6
  423.7 5.5 %collective-permute-done.33 = bf16[128,1536]{1,0:T(8,128)(2,1)S(1)} collective-permute-done((bf16[128,1536]{1,0:T(8,128)(2,1)S(1)}, bf16[128,1536]{1,0:T(8,128)(2,1)S(1)}, u32[]{:S(2)}, u32[]{:S(2)}) %collective-permute-start.33) | collective-permute-done | bytes 393248 | tf_op jit(solution)/shard_map/ppermute | solution.py:1404
  429.2 2.8 convert_add_fusion.3
  432.0 3.0 collective-permute-start.34
  435.0 5.2 %qkv_grads.1 = (bf16[8,96,768]{2,1,0:T(8,128)(2,1)S(1)}, bf16[8,96,768]{2,1,0:T(8,128)(2,1)S(1)}) custom-call(s32[4]{0:T(128)S(1)} %copy-done.8, bf16[1024,1536]{1,0:T(8,128)(2,1)S(1)} %bitcast.84, bf16[2,1024,384]{2,1,0:T(8,128)(2,1)S(1)} %bitcast.78), custom_call_target="tpu_custom_call" | custom-call | flops 5000000000 | bytes 15000000 | tf_op jit(solution)/shard_map/qkv_grads/pallas_call | solution.py:1378
  450.5 3.0 fusion.17
  457.1 3.7 uncut_units.1
  460.8 2.5 copy.39
  471.3 3.7 all-to-all-start.7
  479.7 2.5 all-to-all-done.7
  (258 shorter events, 113.6 us)
Async XLA Ops:
  7.2 74.0 %all-gather.3.cloned.1.call-start = ((), (), s32[]{:S(2)}) async-start(), calls=%async_computation.10 | async-start | bytes 3932160 | tf_op jit(solution)/shard_map/all_gather | solution.py:1478
  7.9 17.4 %collective-permute-start.1 = (bf16[192,384]{1,0:T(8,128)(2,1)}, bf16[192,384]{1,0:T(8,128)(2,1)S(1)}, u32[]{:S(2)}, u32[]{:S(2)}) collective-permute-start(bf16[192,384]{1,0:T(8,128)(2,1)} %bitcast.98), channel_id=1, source_target_pairs={{0,2},{1,3},{2,0},{3,1},{4,6},{5,7},{6,4},{7,5},{8,10},{9,11},{10,... | collective-permute-start | bytes 442376 | tf_op jit(solution)/shard_map/ppermute | solution.py:1409
  12.0 13.3 %collective-permute-start = (bf16[192,384]{1,0:T(8,128)(2,1)}, bf16[192,384]{1,0:T(8,128)(2,1)S(1)}, u32[]{:S(2)}, u32[]{:S(2)}) collective-permute-start(bf16[192,384]{1,0:T(8,128)(2,1)} %bitcast.99), channel_id=1, source_target_pairs={{0,1},{1,2},{2,3},{3,0},{4,5},{5,6},{6,7},{7,4},{8,9},{9,10},{10,1... | collective-permute-start | bytes 442376 | tf_op jit(solution)/shard_map/ppermute | solution.py:1409
  13.6 12.4 %collective-permute-start.2 = (bf16[192,384]{1,0:T(8,128)(2,1)}, bf16[192,384]{1,0:T(8,128)(2,1)S(1)}, u32[]{:S(2)}, u32[]{:S(2)}) collective-permute-start(bf16[192,384]{1,0:T(8,128)(2,1)} %bitcast.100), channel_id=1, source_target_pairs={{0,3},{1,0},{2,1},{3,2},{4,7},{5,4},{6,5},{7,6},{8,11},{9,8},{10,9... | collective-permute-start | bytes 442376 | tf_op jit(solution)/shard_map/ppermute | solution.py:1409
  17.2 39.4 %all-to-all-start = ((f32[32,1,128]{2,1,0:T(1,128)}), f32[32,1,128]{2,1,0:T(1,128)S(1)}, u32[]{:S(2)}, u32[]{:S(2)}) async-start(f32[32,1,128]{2,1,0:T(1,128)} %broadcast_in_dim.47), calls=%async_computation | async-start | bytes 32768 | tf_op jit(solution)/shard_map/all_to_all | solution.py:1458
  26.1 9.8 %collective-permute-start.4 = (bf16[2,192,384]{2,1,0:T(8,128)(2,1)S(1)}, bf16[2,192,384]{2,1,0:T(8,128)(2,1)S(1)}, u32[]{:S(2)}, u32[]{:S(2)}) collective-permute-start(bf16[2,192,384]{2,1,0:T(8,128)(2,1)S(1)} %maximum_bitcast_fusion), channel_id=1, source_target_pairs={{0,16},{16,0},{1,17},{17,1},{2,18},{18,2},{3,19},{19,3},{4,20},{20... | collective-permute-start | bytes 884744 | tf_op jit(solution)/shard_map/ppermute | solution.py:1404
  27.5 9.8 %collective-permute-start.3 = (bf16[2,192,384]{2,1,0:T(8,128)(2,1)S(1)}, bf16[2,192,384]{2,1,0:T(8,128)(2,1)S(1)}, u32[]{:S(2)}, u32[]{:S(2)}) collective-permute-start(bf16[2,192,384]{2,1,0:T(8,128)(2,1)S(1)} %maximum_bitcast_fusion), channel_id=1, source_target_pairs={{0,8},{8,0},{1,9},{9,1},{2,10},{10,2},{3,11},{11,3},{4,12},{12,4},... | collective-permute-start | bytes 884744 | tf_op jit(solution)/shard_map/ppermute | solution.py:1404
  34.6 22.1 %collective-permute-start.9 = (bf16[4,192,384]{2,1,0:T(8,128)(2,1)S(1)}, bf16[4,192,384]{2,1,0:T(8,128)(2,1)S(1)}, u32[]{:S(2)}, u32[]{:S(2)}) collective-permute-start(bf16[4,192,384]{2,1,0:T(8,128)(2,1)S(1)} %pad_maximum_fusion.1), channel_id=1, source_target_pairs={{0,16},{16,0},{1,17},{17,1},{2,18},{18,2},{3,19},{19,3},{4,20},{20... | collective-permute-start | bytes 1769480 | tf_op jit(solution)/shard_map/ppermute | solution.py:1404
  35.2 21.5 %collective-permute-start.8 = (bf16[4,192,384]{2,1,0:T(8,128)(2,1)S(1)}, bf16[4,192,384]{2,1,0:T(8,128)(2,1)}, u32[]{:S(2)}, u32[]{:S(2)}) collective-permute-start(bf16[4,192,384]{2,1,0:T(8,128)(2,1)S(1)} %pad_maximum_fusion.1), channel_id=1, source_target_pairs={{0,8},{8,0},{1,9},{9,1},{2,10},{10,2},{3,11},{11,3},{4,12},{12,4},... | collective-permute-start | bytes 1769480 | tf_op jit(solution)/shard_map/ppermute | solution.py:1404
  35.9 16.7 %collective-permute-start.5 = (bf16[1,192,384]{2,1,0:T(8,128)(2,1)S(1)}, bf16[1,192,384]{2,1,0:T(8,128)(2,1)S(1)}, u32[]{:S(2)}, u32[]{:S(2)}) collective-permute-start(bf16[1,192,384]{2,1,0:T(8,128)(2,1)S(1)} %slice.235), channel_id=1, source_target_pairs={{0,8},{8,0},{1,9},{9,1},{2,10},{10,2},{3,11},{11,3},{4,12},{12,4},... | collective-permute-start | bytes 442376 | tf_op jit(solution)/shard_map/ppermute | solution.py:1404
  37.3 15.3 %collective-permute-start.6 = (bf16[1,192,384]{2,1,0:T(8,128)(2,1)S(1)}, bf16[1,192,384]{2,1,0:T(8,128)(2,1)S(1)}, u32[]{:S(2)}, u32[]{:S(2)}) collective-permute-start(bf16[1,192,384]{2,1,0:T(8,128)(2,1)S(1)} %slice.236), channel_id=1, source_target_pairs={{0,16},{16,0},{1,17},{17,1},{2,18},{18,2},{3,19},{19,3},{4,20},{20... | collective-permute-start | bytes 442376 | tf_op jit(solution)/shard_map/ppermute | solution.py:1404
  52.7 11.8 %collective-permute-start.7 = (bf16[8,192,384]{2,1,0:T(8,128)(2,1)S(1)}, bf16[8,192,384]{2,1,0:T(8,128)(2,1)}, u32[]{:S(2)}, u32[]{:S(2)}) collective-permute-start(bf16[8,192,384]{2,1,0:T(8,128)(2,1)S(1)} %constant_dynamic-update-slice_fusion.mine_ref), channel_id=1, source_target_pairs={{0,4},{4,0},{1,5},{5,1},{2,6},{6,2},{3,7},{7,3},{8,12},{12,8},{9,1... | collective-permute-start | bytes 3538952 | tf_op jit(solution)/shard_map/ppermute | solution.py:1404
  60.1 21.1 %all-to-all-start.1 = ((bf16[8,192,384]{2,1,0:T(8,128)(2,1)}), bf16[8,192,384]{2,1,0:T(8,128)(2,1)}, u32[]{:S(2)}, u32[]{:S(2)}) async-start(bf16[8,192,384]{2,1,0:T(8,128)(2,1)} %cut_units.1), calls=%async_computation.1 | async-start | bytes 2359296 | tf_op jit(solution)/shard_map/all_to_all | solution.py:1458
  64.4 136.7 %all-gather.5.cloned.1.call-start = ((), (), s32[]{:S(2)}) async-start(), calls=%async_computation.11 | async-start | bytes 5898240 | tf_op jit(solution)/shard_map/all_gather | solution.py:1513
  83.4 11.9 %collective-permute-start.11 = (bf16[2,192,384]{2,1,0:T(8,128)(2,1)S(1)}, bf16[2,192,384]{2,1,0:T(8,128)(2,1)S(1)}, u32[]{:S(2)}, u32[]{:S(2)}) collective-permute-start(bf16[2,192,384]{2,1,0:T(8,128)(2,1)S(1)} %slice.186), channel_id=1, source_target_pairs={{0,16},{16,0},{1,17},{17,1},{2,18},{18,2},{3,19},{19,3},{4,20},{20... | collective-permute-start | bytes 884744 | tf_op jit(solution)/shard_map/ppermute | solution.py:1404
  84.0 11.3 %collective-permute-start.10 = (bf16[2,192,384]{2,1,0:T(8,128)(2,1)S(1)}, bf16[2,192,384]{2,1,0:T(8,128)(2,1)S(1)}, u32[]{:S(2)}, u32[]{:S(2)}) collective-permute-start(bf16[2,192,384]{2,1,0:T(8,128)(2,1)S(1)} %slice.185), channel_id=1, source_target_pairs={{0,8},{8,0},{1,9},{9,1},{2,10},{10,2},{3,11},{11,3},{4,12},{12,4},... | collective-permute-start | bytes 884744 | tf_op jit(solution)/shard_map/ppermute | solution.py:1404
  95.2 23.6 %all-to-all-start.2 = ((bf16[4,512,384]{2,1,0:T(8,128)(2,1)}), bf16[4,512,384]{2,1,0:T(8,128)(2,1)S(1)}, u32[]{:S(2)}, u32[]{:S(2)}) async-start(bf16[4,512,384]{2,1,0:T(8,128)(2,1)} %get-tuple-element.116), calls=%async_computation.2 | async-start | bytes 3145728 | tf_op jit(solution)/shard_map/all_to_all | solution.py:1458
  104.2 53.2 %collective-permute-start.14 = (bf16[16,192,384]{2,1,0:T(8,128)(2,1)}, bf16[16,192,384]{2,1,0:T(8,128)(2,1)}, u32[]{:S(2)}, u32[]{:S(2)}) collective-permute-start(bf16[16,192,384]{2,1,0:T(8,128)(2,1)} %constant_dynamic-update-slice_fusion.5.mine_ref), channel_id=1, source_target_pairs={{0,4},{4,0},{1,5},{5,1},{2,6},{6,2},{3,7},{7,3},{8,12},{12,8},{9,1... | collective-permute-start | bytes 7077896 | tf_op jit(solution)/shard_map/ppermute | solution.py:1404
  118.9 22.0 %collective-permute-start.13 = (bf16[256,1536]{1,0:T(8,128)(2,1)S(1)}, bf16[256,1536]{1,0:T(8,128)(2,1)S(1)}, u32[]{:S(2)}, u32[]{:S(2)}) collective-permute-start(bf16[256,1536]{1,0:T(8,128)(2,1)S(1)} %bitcast.81), channel_id=1, source_target_pairs={{0,16},{16,0},{1,17},{17,1},{2,18},{18,2},{3,19},{19,3},{4,20},{20... | collective-permute-start | bytes 2359304 | tf_op jit(solution)/shard_map/ppermute | solution.py:1404
  120.3 20.6 %collective-permute-start.12 = (bf16[256,1536]{1,0:T(8,128)(2,1)S(1)}, bf16[256,1536]{1,0:T(8,128)(2,1)S(1)}, u32[]{:S(2)}, u32[]{:S(2)}) collective-permute-start(bf16[256,1536]{1,0:T(8,128)(2,1)S(1)} %bitcast.82), channel_id=1, source_target_pairs={{0,8},{8,0},{1,9},{9,1},{2,10},{10,2},{3,11},{11,3},{4,12},{12,4},... | collective-permute-start | bytes 2359304 | tf_op jit(solution)/shard_map/ppermute | solution.py:1404
  142.7 52.3 %all-to-all-start.3 = ((bf16[16,64,384]{2,1,0:T(8,128)(2,1)}), bf16[16,64,384]{2,1,0:T(8,128)(2,1)S(1)}, u32[]{:S(2)}, u32[]{:S(2)}) async-start(bf16[16,64,384]{2,1,0:T(8,128)(2,1)} %get-tuple-element.119), calls=%async_computation.3 | async-start | bytes 1572864 | tf_op jit(solution)/shard_map/all_to_all | solution.py:1458
  157.3 249.7 %reduce-scatter.3.cloned.1.call-start = ((), (), s32[]{:S(2)}) async-start(), calls=%async_computation.12 | async-start | bytes 5898240 | tf_op jit(solution)/shard_map/reduce_scatter | solution.py:1551
  162.5 11.5 %collective-permute-start.16 = (bf16[128,1536]{1,0:T(8,128)(2,1)S(1)}, bf16[128,1536]{1,0:T(8,128)(2,1)S(1)}, u32[]{:S(2)}, u32[]{:S(2)}) collective-permute-start(bf16[128,1536]{1,0:T(8,128)(2,1)S(1)} %slice.188), channel_id=1, source_target_pairs={{0,16},{16,0},{1,17},{17,1},{2,18},{18,2},{3,19},{19,3},{4,20},{20... | collective-permute-start | bytes 1179656 | tf_op jit(solution)/shard_map/ppermute | solution.py:1404
  163.3 14.7 %collective-permute-start.15 = (bf16[128,1536]{1,0:T(8,128)(2,1)S(1)}, bf16[128,1536]{1,0:T(8,128)(2,1)S(1)}, u32[]{:S(2)}, u32[]{:S(2)}) collective-permute-start(bf16[128,1536]{1,0:T(8,128)(2,1)S(1)} %slice.187), channel_id=1, source_target_pairs={{0,8},{8,0},{1,9},{9,1},{2,10},{10,2},{3,11},{11,3},{4,12},{12,4},... | collective-permute-start | bytes 1179656 | tf_op jit(solution)/shard_map/ppermute | solution.py:1404
  201.1 20.0 %collective-permute-start.18 = (bf16[256,1536]{1,0:T(8,128)(2,1)S(1)}, bf16[256,1536]{1,0:T(8,128)(2,1)S(1)}, u32[]{:S(2)}, u32[]{:S(2)}) collective-permute-start(bf16[256,1536]{1,0:T(8,128)(2,1)S(1)} %get-tuple-element.129.refs_0_), channel_id=1, source_target_pairs={{0,16},{16,0},{1,17},{17,1},{2,18},{18,2},{3,19},{19,3},{4,20},{20... | collective-permute-start | bytes 2359304 | tf_op jit(solution)/shard_map/ppermute | solution.py:1404
  202.6 19.8 %collective-permute-start.17 = (bf16[256,1536]{1,0:T(8,128)(2,1)S(1)}, bf16[256,1536]{1,0:T(8,128)(2,1)}, u32[]{:S(2)}, u32[]{:S(2)}) collective-permute-start(bf16[256,1536]{1,0:T(8,128)(2,1)S(1)} %get-tuple-element.129.refs_0_), channel_id=1, source_target_pairs={{0,8},{8,0},{1,9},{9,1},{2,10},{10,2},{3,11},{11,3},{4,12},{12,4},... | collective-permute-start | bytes 2359304 | tf_op jit(solution)/shard_map/ppermute | solution.py:1404
  223.4 25.5 %collective-permute-start.20 = (bf16[128,1536]{1,0:T(8,128)(2,1)S(1)}, bf16[128,1536]{1,0:T(8,128)(2,1)S(1)}, u32[]{:S(2)}, u32[]{:S(2)}) collective-permute-start(bf16[128,1536]{1,0:T(8,128)(2,1)S(1)} %slice.190), channel_id=1, source_target_pairs={{0,8},{8,0},{1,9},{9,1},{2,10},{10,2},{3,11},{11,3},{4,12},{12,4},... | collective-permute-start | bytes 1179656 | tf_op jit(solution)/shard_map/ppermute | solution.py:1404
  224.0 24.9 %collective-permute-start.21 = (bf16[128,1536]{1,0:T(8,128)(2,1)S(1)}, bf16[128,1536]{1,0:T(8,128)(2,1)}, u32[]{:S(2)}, u32[]{:S(2)}) collective-permute-start(bf16[128,1536]{1,0:T(8,128)(2,1)S(1)} %slice.191), channel_id=1, source_target_pairs={{0,16},{16,0},{1,17},{17,1},{2,18},{18,2},{3,19},{19,3},{4,20},{20... | collective-permute-start | bytes 1179656 | tf_op jit(solution)/shard_map/ppermute | solution.py:1404
  245.9 34.0 %collective-permute-start.22 = (bf16[128,1536]{1,0:T(8,128)(2,1)}, bf16[128,1536]{1,0:T(8,128)(2,1)S(1)}, u32[]{:S(2)}, u32[]{:S(2)}) collective-permute-start(bf16[128,1536]{1,0:T(8,128)(2,1)} %get-tuple-element.140), channel_id=1, source_target_pairs={{0,8},{8,0},{1,9},{9,1},{2,10},{10,2},{3,11},{11,3},{4,12},{12,4},... | collective-permute-start | bytes 1179656 | tf_op jit(solution)/shard_map/ppermute | solution.py:1404
  247.4 32.4 %collective-permute-start.23 = (bf16[128,1536]{1,0:T(8,128)(2,1)}, bf16[128,1536]{1,0:T(8,128)(2,1)S(1)}, u32[]{:S(2)}, u32[]{:S(2)}) collective-permute-start(bf16[128,1536]{1,0:T(8,128)(2,1)} %get-tuple-element.141), channel_id=1, source_target_pairs={{0,16},{16,0},{1,17},{17,1},{2,18},{18,2},{3,19},{19,3},{4,20},{20... | collective-permute-start | bytes 1179656 | tf_op jit(solution)/shard_map/ppermute | solution.py:1404
  259.4 20.4 %collective-permute-start.24 = (bf16[128,1536]{1,0:T(8,128)(2,1)}, bf16[128,1536]{1,0:T(8,128)(2,1)S(1)}, u32[]{:S(2)}, u32[]{:S(2)}) collective-permute-start(bf16[128,1536]{1,0:T(8,128)(2,1)} %get-tuple-element.142), channel_id=1, source_target_pairs={{0,8},{8,0},{1,9},{9,1},{2,10},{10,2},{3,11},{11,3},{4,12},{12,4},... | collective-permute-start | bytes 1179656 | tf_op jit(solution)/shard_map/ppermute | solution.py:1404
  260.1 19.8 %collective-permute-start.25 = (bf16[128,1536]{1,0:T(8,128)(2,1)}, bf16[128,1536]{1,0:T(8,128)(2,1)S(1)}, u32[]{:S(2)}, u32[]{:S(2)}) collective-permute-start(bf16[128,1536]{1,0:T(8,128)(2,1)} %get-tuple-element.143), channel_id=1, source_target_pairs={{0,16},{16,0},{1,17},{17,1},{2,18},{18,2},{3,19},{19,3},{4,20},{20... | collective-permute-start | bytes 1179656 | tf_op jit(solution)/shard_map/ppermute | solution.py:1404
  281.5 12.1 %collective-permute-start.28 = (bf16[128,1536]{1,0:T(8,128)(2,1)S(1)}, bf16[128,1536]{1,0:T(8,128)(2,1)S(1)}, u32[]{:S(2)}, u32[]{:S(2)}) collective-permute-start(bf16[128,1536]{1,0:T(8,128)(2,1)S(1)} %get-tuple-element.230), channel_id=1, source_target_pairs={{0,16},{16,0},{1,17},{17,1},{2,18},{18,2},{3,19},{19,3},{4,20},{20... | collective-permute-start | bytes 1179656 | tf_op jit(solution)/shard_map/ppermute | solution.py:1404
  283.1 11.2 %collective-permute-start.27 = (bf16[128,1536]{1,0:T(8,128)(2,1)S(1)}, bf16[128,1536]{1,0:T(8,128)(2,1)S(1)}, u32[]{:S(2)}, u32[]{:S(2)}) collective-permute-start(bf16[128,1536]{1,0:T(8,128)(2,1)S(1)} %get-tuple-element.231), channel_id=1, source_target_pairs={{0,8},{8,0},{1,9},{9,1},{2,10},{10,2},{3,11},{11,3},{4,12},{12,4},... | collective-permute-start | bytes 1179656 | tf_op jit(solution)/shard_map/ppermute | solution.py:1404
  309.2 20.1 %collective-permute-start.29 = (bf16[8,96,1536]{2,1,0:T(8,128)(2,1)}, bf16[8,96,1536]{2,1,0:T(8,128)(2,1)}, u32[]{:S(2)}, u32[]{:S(2)}) collective-permute-start(bf16[8,96,1536]{2,1,0:T(8,128)(2,1)} %get-tuple-element.166), channel_id=1, source_target_pairs={{0,4},{4,0},{1,5},{5,1},{2,6},{6,2},{3,7},{7,3},{8,12},{12,8},{9,1... | collective-permute-start | bytes 7077896 | tf_op jit(solution)/shard_map/ppermute | solution.py:1404
  309.2 45.3 %all-to-all-start.4 = ((bf16[16,64,384]{2,1,0:T(8,128)(2,1)}), bf16[16,64,384]{2,1,0:T(8,128)(2,1)}, u32[]{:S(2)}, u32[]{:S(2)}) async-start(bf16[16,64,384]{2,1,0:T(8,128)(2,1)} %copy-done.6), calls=%async_computation.4 | async-start | bytes 1572864 | tf_op jit(solution)/shard_map/all_to_all | solution.py:1458
  326.9 56.5 %collective-permute-start.31 = (bf16[256,1536]{1,0:T(8,128)(2,1)}, bf16[256,1536]{1,0:T(8,128)(2,1)}, u32[]{:S(2)}, u32[]{:S(2)}) collective-permute-start(bf16[256,1536]{1,0:T(8,128)(2,1)} %get-tuple-element.167), channel_id=1, source_target_pairs={{0,8},{8,0},{1,9},{9,1},{2,10},{10,2},{3,11},{11,3},{4,12},{12,4},... | collective-permute-start | bytes 2359304 | tf_op jit(solution)/shard_map/ppermute | solution.py:1404
  328.5 54.9 %collective-permute-start.32 = (bf16[256,1536]{1,0:T(8,128)(2,1)}, bf16[256,1536]{1,0:T(8,128)(2,1)}, u32[]{:S(2)}, u32[]{:S(2)}) collective-permute-start(bf16[256,1536]{1,0:T(8,128)(2,1)} %get-tuple-element.168), channel_id=1, source_target_pairs={{0,16},{16,0},{1,17},{17,1},{2,18},{18,2},{3,19},{19,3},{4,20},{20... | collective-permute-start | bytes 2359304 | tf_op jit(solution)/shard_map/ppermute | solution.py:1404
  333.8 49.5 %collective-permute-start.30 = (bf16[384,1536]{1,0:T(8,128)(2,1)S(1)}, bf16[384,1536]{1,0:T(8,128)(2,1)S(1)}, u32[]{:S(2)}, u32[]{:S(2)}) collective-permute-start(bf16[384,1536]{1,0:T(8,128)(2,1)S(1)} %bitcast.93), channel_id=1, source_target_pairs={{0,8},{8,0},{1,9},{9,1},{2,10},{10,2},{3,11},{11,3},{4,12},{12,4},... | collective-permute-start | bytes 3538952 | tf_op jit(solution)/shard_map/ppermute | solution.py:1404
  383.4 23.6 %all-to-all-start.5 = ((bf16[4,512,384]{2,1,0:T(8,128)(2,1)}), bf16[4,512,384]{2,1,0:T(8,128)(2,1)S(1)}, u32[]{:S(2)}, u32[]{:S(2)}) async-start(bf16[4,512,384]{2,1,0:T(8,128)(2,1)} %bitcast.90), calls=%async_computation.5 | async-start | bytes 3145728 | tf_op jit(solution)/shard_map/all_to_all | solution.py:1458
  386.9 97.2 %reduce-scatter.5.cloned.1.call-start = ((), (), s32[]{:S(2)}) async-start(), calls=%async_computation.13 | async-start | bytes 4669440 | tf_op jit(solution)/shard_map/reduce_scatter | solution.py:1575
  389.0 15.7 %collective-permute-start.35 = (bf16[192,1536]{1,0:T(8,128)(2,1)S(1)}, bf16[192,1536]{1,0:T(8,128)(2,1)S(1)}, u32[]{:S(2)}, u32[]{:S(2)}) collective-permute-start(bf16[192,1536]{1,0:T(8,128)(2,1)S(1)} %slice.296), channel_id=1, source_target_pairs={{0,16},{16,0},{1,17},{17,1},{2,18},{18,2},{3,19},{19,3},{4,20},{20... | collective-permute-start | bytes 1769480 | tf_op jit(solution)/shard_map/ppermute | solution.py:1404
  417.1 12.1 %collective-permute-start.33 = (bf16[128,1536]{1,0:T(8,128)(2,1)S(1)}, bf16[128,1536]{1,0:T(8,128)(2,1)S(1)}, u32[]{:S(2)}, u32[]{:S(2)}) collective-permute-start(bf16[128,1536]{1,0:T(8,128)(2,1)S(1)} %add_convert_fusion.2), channel_id=1, source_target_pairs={{0,16},{16,0},{1,17},{17,1},{2,18},{18,2},{3,19},{19,3},{4,20},{20... | collective-permute-start | bytes 1179656 | tf_op jit(solution)/shard_map/ppermute | solution.py:1404
  418.9 22.4 %all-to-all-start.6 = ((bf16[8,192,384]{2,1,0:T(8,128)(2,1)}), bf16[8,192,384]{2,1,0:T(8,128)(2,1)}, u32[]{:S(2)}, u32[]{:S(2)}) async-start(bf16[8,192,384]{2,1,0:T(8,128)(2,1)} %bitcast.38), calls=%async_computation.8 | async-start | bytes 2359296 | tf_op jit(solution)/shard_map/all_to_all | solution.py:1458
  432.0 15.5 %collective-permute-start.34 = (bf16[128,1536]{1,0:T(8,128)(2,1)}, bf16[128,1536]{1,0:T(8,128)(2,1)}, u32[]{:S(2)}, u32[]{:S(2)}) collective-permute-start(bf16[128,1536]{1,0:T(8,128)(2,1)} %get-tuple-element.229), channel_id=1, source_target_pairs={{0,8},{8,0},{1,9},{9,1},{2,10},{10,2},{3,11},{11,3},{4,12},{12,4},... | collective-permute-start | bytes 1179656 | tf_op jit(solution)/shard_map/ppermute | solution.py:1404
  441.3 9.2 %collective-permute-start.36 = (bf16[8,96,768]{2,1,0:T(8,128)(2,1)}, bf16[8,96,768]{2,1,0:T(8,128)(2,1)}, u32[]{:S(2)}, u32[]{:S(2)}) collective-permute-start(bf16[8,96,768]{2,1,0:T(8,128)(2,1)} %copy-done.9), channel_id=1, source_target_pairs={{0,4},{4,0},{1,5},{5,1},{2,6},{6,2},{3,7},{7,3},{8,12},{12,8},{9,1... | collective-permute-start | bytes 3538952 | tf_op jit(solution)/shard_map/ppermute | solution.py:1404
  454.4 8.9 %collective-permute-start.37 = (bf16[192,768]{1,0:T(8,128)(2,1)}, bf16[192,768]{1,0:T(8,128)(2,1)S(1)}, u32[]{:S(2)}, u32[]{:S(2)}) collective-permute-start(bf16[192,768]{1,0:T(8,128)(2,1)} %bitcast.41), channel_id=1, source_target_pairs={{0,8},{8,0},{1,9},{9,1},{2,10},{10,2},{3,11},{11,3},{4,12},{12,4},... | collective-permute-start | bytes 884744 | tf_op jit(solution)/shard_map/ppermute | solution.py:1404
  471.3 10.9 %all-to-all-start.7 = ((f32[32,1,128]{2,1,0:T(1,128)}), f32[32,1,128]{2,1,0:T(1,128)S(1)}, u32[]{:S(2)}, u32[]{:S(2)}) async-start(f32[32,1,128]{2,1,0:T(1,128)} %bitcast.45), calls=%async_computation.9 | async-start | bytes 32768 | tf_op jit(solution)/shard_map/all_to_all | solution.py:1458
  (52 other events, 610.2 us)
Sparse Core Ops, SparseCore 0:
  9.6 67.6 all-gather.2
  81.3 113.7 all-gather.4
  295.2 95.3 reduce-scatter.2
  415.9 68.1 reduce-scatter.4
where the time goes:
time: 498 us; the launch traced here: 496 us
  Pallas kernels  167 us (34%)
  waiting for transfers between devices  136 us (27%)
  starting transfers between devices  87.5 us (18%)
  local copies, waits for them, and re-layouts  49 us (10%)
  other arithmetic  41.3 us (8%)
  between operations  15.2 us (3%)
    all_to_all x8, waiting for transfers between devices, all_to_all(): return lax.all_to_all(value, axes, 0, 0, tiled=True)  69.7 us
    ppermute x38, waiting for transfers between devices, swap(): return lax.ppermute(value, axis, SWAP)  63.9 us
    all_to_all x8, starting transfers between devices, all_to_all(): return lax.all_to_all(value, axes, 0, 0, tiled=True)  41.3 us
    ppermute x38, starting transfers between devices, swap(): return lax.ppermute(value, axis, SWAP)  38.1 us
    unnamed x106, local copies, waits for them, and re-layouts  31.7 us
    pallas_call x2, Pallas kernels, units_call(): pl.pallas_call(partial(units_kernel, count, 3 * count if corner else 0, c...  31.1 us
    pallas_call x1, Pallas kernels, attn_bwd(): pl.pallas_call(functools.partial(attn_bwd_kernel, length), grid=(blocks,)...  27.4 us
    pallas_call x1, Pallas kernels, unit_grads_call(): pl.pallas_call(unit_grads_kernel, grid=(parts,), in_specs=[full_spec(v) f...  19.2 us
  transfers between devices with their start and end apart: 53, of which 22 were waited for; matrix products, arithmetic and copies ran while one was open for 13% of the time, Pallas kernels for 32%

commit v1 on v0

--- a/solution.py
+++ b/solution.py
@@ -1231,7 +1231,7 @@
         shapes += [jax.ShapeDtypeStruct((2 * count, width), jnp.float32)]
     shapes += [jax.ShapeDtypeStruct((count // 2, width), low)] * 2
     return pl.pallas_call(
-        partial(units_kernel, count, 3 * count if corner else 0, count),
+        partial(units_kernel, count, 3 * count if corner else 0, count if corner else 3 * count // 2),
         grid=(parts,),
         in_specs=[full_spec(v) for v in pieces] + [unit_spec(mine), unit_spec(other), unit_spec(grad_hidden)],
         out_specs=[

time: 498 us -> 496 us (level)
  no operation moved by 1% of the time
where the time goes in v1:
time: 496 us; the launch traced here: 495 us
  Pallas kernels  165 us (33%)
  waiting for transfers between devices  136 us (27%)
  starting transfers between devices  87.4 us (18%)
  local copies, waits for them, and re-layouts  49 us (10%)
  other arithmetic  41.3 us (8%)
  between operations  15.2 us (3%)
    all_to_all x8, waiting for transfers between devices, all_to_all(): return lax.all_to_all(value, axes, 0, 0, tiled=True)  69.7 us
    ppermute x38, waiting for transfers between devices, swap(): return lax.ppermute(value, axis, SWAP)  63.9 us
    all_to_all x8, starting transfers between devices, all_to_all(): return lax.all_to_all(value, axes, 0, 0, tiled=True)  41.3 us
    ppermute x38, starting transfers between devices, swap(): return lax.ppermute(value, axis, SWAP)  38.1 us
    unnamed x106, local copies, waits for them, and re-layouts  31.7 us
    pallas_call x2, Pallas kernels, units_call(): pl.pallas_call(partial(units_kernel, count, 3 * count if corner else 0, c...  29.9 us
    pallas_call x1, Pallas kernels, attn_bwd(): pl.pallas_call(functools.partial(attn_bwd_kernel, length), grid=(blocks,)...  27.4 us
    pallas_call x1, Pallas kernels, unit_grads_call(): pl.pallas_call(unit_grads_kernel, grid=(parts,), in_specs=[full_spec(v) f...  19.2 us
  transfers between devices with their start and end apart: 53, of which 22 were waited for; matrix products, arithmetic and copies ran while one was open for 13% of the time, Pallas kernels for 32%

profile of v1, /device:TPU:0, one launch (start us, length us, event | category | flops | bytes accessed | tf_op | source)
XLA Modules:
  0.0 494.5 jit_solution(10082336032195432246)
XLA Ops:
  7.9 4.1 collective-permute-start.1
  13.6 2.2 collective-permute-start.2
  17.2 2.8 all-to-all-start
  29.1 5.6 %multiply_sine_fusion = (f32[2048,128]{1,0:T(8,128)}, f32[2048,128]{1,0:T(8,128)}) fusion(f32[128]{0:T(128)S(1)} %fusion.15, f32[2048]{0:T(1024)S(1)} %subtract_convert_fusion), kind=kLoop, calls=%fused_computation.14 | loop fusion | flops 262144 | bytes 2105856 | tf_op jit(solution)/shard_map/sin | solution.py:1500
  39.1 13.6 %collective-permute-done.5 = bf16[1,192,384]{2,1,0:T(8,128)(2,1)S(1)} collective-permute-done((bf16[1,192,384]{2,1,0:T(8,128)(2,1)S(1)}, bf16[1,192,384]{2,1,0:T(8,128)(2,1)S(1)}, u32[]{:S(2)}, u32[]{:S(2)}) %collective-permute-start.5) | collective-permute-done | bytes 147488 | tf_op jit(solution)/shard_map/ppermute | solution.py:1404
  56.7 3.4 cut_units.1
  60.1 4.3 all-to-all-start.1
  67.4 13.8 %all-to-all-done.1 = bf16[8,192,384]{2,1,0:T(8,128)(2,1)} async-done(((bf16[8,192,384]{2,1,0:T(8,128)(2,1)}), bf16[8,192,384]{2,1,0:T(8,128)(2,1)}, u32[]{:S(2)}, u32[]{:S(2)}) %all-to-all-start.1) | async-done | bytes 1179680 | tf_op jit(solution)/shard_map/all_to_all | solution.py:1458
  86.3 9.0 %norm_qkv.1 = (bf16[2,512,1536]{2,1,0:T(8,128)(2,1)}, bf16[4,512,384]{2,1,0:T(8,128)(2,1)}) custom-call(bf16[1024,1536]{1,0:T(8,128)(2,1)} %all-gather.3.cloned.1.call-done.h_ref, f32[1,1536]{1,0:T(1,128)S(1)} %reshape.188.gain_ref, bf16[1536,768]{1,0:T(8,128)(2,1)S(1)} %copy-done.20, f32[2,512,128]{2,1,0:T(8,128)S(1)} %get-tuple-element.111.cos_ref, ...), custom_call_target="tpu_custom_call" | custom-call | flops 7000000000 | bytes 21000000 | tf_op jit(solution)/shard_map/norm_qkv/pallas_call | solution.py:839
  95.2 3.6 all-to-all-start.2
  104.6 14.3 %all-to-all-done.2 = bf16[4,512,384]{2,1,0:T(8,128)(2,1)S(1)} async-done(((bf16[4,512,384]{2,1,0:T(8,128)(2,1)}), bf16[4,512,384]{2,1,0:T(8,128)(2,1)S(1)}, u32[]{:S(2)}, u32[]{:S(2)}) %all-to-all-start.2) | async-done | bytes 1572896 | tf_op jit(solution)/shard_map/all_to_all | solution.py:1458
  120.7 18.2 %attend.1 = (bf16[16,64,384]{2,1,0:T(8,128)(2,1)}, f32[8,512,128]{2,1,0:T(8,128)S(1)}, f32[8,8,512]{2,1,0:T(8,128)S(1)}) custom-call(s32[1]{0:T(128)} %bitcast.first_ref, bf16[2048,384]{1,0:T(8,128)(2,1)S(1)} %bitcast.75), custom_call_target="tpu_custom_call" | custom-call | flops 22000001024 | bytes 66000000 | tf_op jit(solution)/shard_map/attend/pallas_call | solution.py:647
  142.7 14.6 %all-to-all-start.3 = ((bf16[16,64,384]{2,1,0:T(8,128)(2,1)}), bf16[16,64,384]{2,1,0:T(8,128)(2,1)S(1)}, u32[]{:S(2)}, u32[]{:S(2)}) async-start(bf16[16,64,384]{2,1,0:T(8,128)(2,1)} %get-tuple-element.119), calls=%async_computation.3 | async-start | bytes 1572864 | tf_op jit(solution)/shard_map/all_to_all | solution.py:1458
  157.4 2.9 place_out.3.w_ref
  160.3 2.2 copy-done.18
  165.3 8.8 %collective-permute-done.16.refs_4_.refs_9_ = bf16[128,1536]{1,0:T(8,128)(2,1)S(1)} collective-permute-done((bf16[128,1536]{1,0:T(8,128)(2,1)S(1)}, bf16[128,1536]{1,0:T(8,128)(2,1)S(1)}, u32[]{:S(2)}, u32[]{:S(2)}) %collective-permute-start.16) | collective-permute-done | bytes 393248 | tf_op jit(solution)/shard_map/ppermute | solution.py:1404
  174.0 3.9 collective-permute-done.15.refs_3_.refs_8_
  177.9 17.0 %all-to-all-done.3.o_ref = bf16[16,64,384]{2,1,0:T(8,128)(2,1)S(1)} async-done(((bf16[16,64,384]{2,1,0:T(8,128)(2,1)}), bf16[16,64,384]{2,1,0:T(8,128)(2,1)S(1)}, u32[]{:S(2)}, u32[]{:S(2)}) %all-to-all-start.3) | async-done | bytes 786464 | tf_op jit(solution)/shard_map/all_to_all | solution.py:1458
  195.0 4.0 out_norm.1
  203.3 6.0 %collective-permute-done.19.refs_6_.refs_4_.refs_3_.w1_ref = bf16[4,1536,384]{2,1,0:T(8,128)(2,1)} collective-permute-done((bf16[4,1536,384]{2,1,0:T(8,128)(2,1)}, bf16[4,1536,384]{2,1,0:T(8,128)(2,1)}, u32[]{:S(2)}, u32[]{:S(2)}) %collective-permute-start.19) | collective-permute-done | bytes 4718624 | tf_op jit(solution)/shard_map/ppermute | solution.py:1404
  209.3 9.6 %down_back.1.refs_5_.refs_4_ = f32[4,1024,256]{2,1,0:T(8,128)} custom-call(bf16[256,1536]{1,0:T(8,128)(2,1)} %bitcast.79, bf16[256,1536]{1,0:T(8,128)(2,1)} %copy-done.32, bf16[256,1536]{1,0:T(8,128)(2,1)} %copy-done.30, bf16[128,1536]{1,0:T(8,128)(2,1)} %copy-done.45, bf16[128,1536]{1,0:T(8,128)(2,1)} %copy-done.44, bf16[4,1536,384]{2,1,0:T(8,128)(2,1)} %bitcast.108, ...), custom_call_target="tpu_custom_call" | custom-call | flops 8000000000 | bytes 24000000 | tf_op jit(solution)/shard_map/down_back/pallas_call | solution.py:1153
  218.9 2.1 collective-permute-done.18.refs_2_
  224.6 20.1 %units.1 = (bf16[4,2,768,256]{3,2,1,0:T(8,128)(2,1)}, bf16[4,768,256]{2,1,0:T(8,128)(2,1)}, f32[512,1536]{1,0:T(8,128)}, bf16[128,1536]{1,0:T(8,128)(2,1)}, bf16[128,1536]{1,0:T(8,128)(2,1)}) custom-call(bf16[256,1536]{1,0:T(8,128)(2,1)} %copy-done.12, bf16[256,1536]{1,0:T(8,128)(2,1)} %collective-permute-done.17.refs_1_, bf16[256,1536]{1,0:T(8,128)(2,1)} %copy-done.34, ...), custom_call_target="tpu_custom_call" | custom-call | flops 19000000512 | bytes 57000000 | tf_op jit(solution)/shard_map/units/pallas_call | solution.py:1233
  248.4 9.8 %units_corner.1 = (bf16[4,2,256,256]{3,2,1,0:T(8,128)(2,1)}, bf16[4,256,256]{2,1,0:T(8,128)(2,1)}, bf16[128,1536]{1,0:T(8,128)(2,1)}, bf16[128,1536]{1,0:T(8,128)(2,1)}) custom-call(bf16[128,1536]{1,0:T(8,128)(2,1)} %copy-done.46, bf16[128,1536]{1,0:T(8,128)(2,1)} %collective-permute-done.21.refs_1_.refs_4_, bf16[4,1536,384]{2,1,0:T(8,128)(2,1)} %bitcast.110, ...), custom_call_target="tpu_custom_call" | custom-call | flops 8000000000 | bytes 24000000 | tf_op jit(solution)/shard_map/units_corner/pallas_call | solution.py:1233
  259.4 19.2 %unit_grads.1 = (bf16[4,1536,384]{2,1,0:T(8,128)(2,1)}, bf16[4,1536,384]{2,1,0:T(8,128)(2,1)}) custom-call(bf16[256,1536]{1,0:T(8,128)(2,1)} %copy-done.12, bf16[256,1536]{1,0:T(8,128)(2,1)} %collective-permute-done.17.refs_1_, bf16[256,1536]{1,0:T(8,128)(2,1)} %copy-done.34, bf16[128,1536]{1,0:T(8,128)(2,1)} %copy-done.46, ...), custom_call_target="tpu_custom_call" | custom-call | flops 19000000512 | bytes 57000000 | tf_op jit(solution)/shard_map/unit_grads/pallas_call | solution.py:1334
  283.3 3.5 collective-permute-done.26
  286.8 5.6 %add_convert_fusion = bf16[4,1536,384]{2,1,0:T(8,128)(2,1)} fusion(bf16[4,1536,384]{2,1,0:T(8,128)(2,1)S(1)} %collective-permute-done.26, bf16[4,1536,384]{2,1,0:T(8,128)(2,1)} %get-tuple-element.149), kind=kLoop, calls=%fused_computation | loop fusion | flops 9437184 | bytes 14155776 | tf_op jit(solution)/shard_map/convert_element_type | solution.py:1548
  296.0 6.4 %mid_back.1 = (f32[256,1536]{1,0:T(8,128)S(1)}, bf16[256,1536]{1,0:T(8,128)(2,1)S(1)}, bf16[16,64,384]{2,1,0:T(8,128)(2,1)S(1)}, f32[1,1536]{1,0:T(1,128)S(1)}) custom-call(f32[512,1536]{1,0:T(8,128)} %get-tuple-element.139.keep_ref, bf16[128,1536]{1,0:T(8,128)(2,1)S(1)} %collective-permute-done.22.fx_ref, ...), custom_call_target="tpu_custom_call" | custom-call | flops 5000000000 | bytes 15000000 | tf_op jit(solution)/shard_map/mid_back/pallas_call | solution.py:964
  303.3 4.6 out_grads.1
  307.9 4.5 all-to-all-start.4
  312.5 13.2 %down.1 = (f32[512,1536]{1,0:T(8,128)}, bf16[256,1536]{1,0:T(8,128)(2,1)}, bf16[256,1536]{1,0:T(8,128)(2,1)}) custom-call(bf16[4,768,256]{2,1,0:T(8,128)(2,1)} %get-tuple-element.156.refs_12_.hid_ref, bf16[4,256,256]{2,1,0:T(8,128)(2,1)} %get-tuple-element.157.refs_13_.hid_last_ref, bf16[4,1536,384]{2,1,0:T(8,128)(2,1)} %bitcast.111, ...), custom_call_target="tpu_custom_call" | custom-call | flops 11000000512 | bytes 33000000 | tf_op jit(solution)/shard_map/down/pallas_call | solution.py:1289
  328.0 2.3 convert_add_fusion
  330.3 2.2 copy-done.24
  333.2 20.1 %all-to-all-done.4.do_ref = bf16[16,64,384]{2,1,0:T(8,128)(2,1)} async-done(((bf16[16,64,384]{2,1,0:T(8,128)(2,1)}), bf16[16,64,384]{2,1,0:T(8,128)(2,1)}, u32[]{:S(2)}, u32[]{:S(2)}) %all-to-all-start.4) | async-done | bytes 786464 | tf_op jit(solution)/shard_map/all_to_all | solution.py:1458
  353.2 27.4 %attend_back.1 = bf16[2048,384]{1,0:T(8,128)(2,1)} custom-call(s32[1]{0:T(128)} %bitcast.first_ref, bf16[2048,384]{1,0:T(8,128)(2,1)} %bitcast.76, bf16[16,64,384]{2,1,0:T(8,128)(2,1)} %all-to-all-done.4.do_ref, f32[8,512,128]{2,1,0:T(8,128)} %copy-done.22, f32[8,8,512]{2,1,0:T(8,128)} %copy-done.23, f32[2048,128]{1,0:T(8,128)} %get-tuple-element.162.cos_ref, ...), custom_call_target="tpu_custom_call" | custom-call | flops 31000000512 | bytes 93000000 | tf_op jit(solution)/shard_map/attend_back/pallas_call | solution.py:754
  382.2 3.6 all-to-all-start.5
  389.4 14.2 %collective-permute-done.35 = bf16[192,1536]{1,0:T(8,128)(2,1)S(1)} collective-permute-done((bf16[192,1536]{1,0:T(8,128)(2,1)S(1)}, bf16[192,1536]{1,0:T(8,128)(2,1)S(1)}, u32[]{:S(2)}, u32[]{:S(2)}) %collective-permute-start.35) | collective-permute-done | bytes 589856 | tf_op jit(solution)/shard_map/ppermute | solution.py:1404
  407.5 7.1 %da_part.1 = (bf16[4,304,1536]{2,1,0:T(8,128)(2,1)}, f32[1,1536]{1,0:T(1,128)S(1)}) custom-call(bf16[1024,1536]{1,0:T(8,128)(2,1)} %all-gather.3.cloned.1.call-done.h_ref, bf16[2,2,512,384]{3,2,1,0:T(8,128)(2,1)S(1)} %bitcast.77, bf16[1536,768]{1,0:T(8,128)(2,1)S(1)} %copy-done.21, bf16[192,1536]{1,0:T(8,128)(2,1)S(1)} %fusion.4.wo_ref), custom_call_target="tpu_custom_call" | custom-call | flops 6000000000 | bytes 18000000 | tf_op jit(solution)/shard_map/da_part/pallas_call | solution.py:1010
  417.7 4.3 all-to-all-start.6
  422.5 5.5 %collective-permute-done.33 = bf16[128,1536]{1,0:T(8,128)(2,1)S(1)} collective-permute-done((bf16[128,1536]{1,0:T(8,128)(2,1)S(1)}, bf16[128,1536]{1,0:T(8,128)(2,1)S(1)}, u32[]{:S(2)}, u32[]{:S(2)}) %collective-permute-start.33) | collective-permute-done | bytes 393248 | tf_op jit(solution)/shard_map/ppermute | solution.py:1404
  428.0 2.8 convert_add_fusion.3
  430.8 3.0 collective-permute-start.34
  433.8 5.2 %qkv_grads.1 = (bf16[8,96,768]{2,1,0:T(8,128)(2,1)S(1)}, bf16[8,96,768]{2,1,0:T(8,128)(2,1)S(1)}) custom-call(s32[4]{0:T(128)S(1)} %copy-done.8, bf16[1024,1536]{1,0:T(8,128)(2,1)S(1)} %bitcast.84, bf16[2,1024,384]{2,1,0:T(8,128)(2,1)S(1)} %bitcast.78), custom_call_target="tpu_custom_call" | custom-call | flops 5000000000 | bytes 15000000 | tf_op jit(solution)/shard_map/qkv_grads/pallas_call | solution.py:1378
  449.3 3.0 fusion.17
  455.9 3.7 uncut_units.1
  459.6 2.5 copy.39
  470.1 3.7 all-to-all-start.7
  478.5 2.5 all-to-all-done.7
  (258 shorter events, 113.6 us)
Async XLA Ops:
  7.2 74.0 %all-gather.3.cloned.1.call-start = ((), (), s32[]{:S(2)}) async-start(), calls=%async_computation.10 | async-start | bytes 3932160 | tf_op jit(solution)/shard_map/all_gather | solution.py:1478
  7.9 17.4 %collective-permute-start.1 = (bf16[192,384]{1,0:T(8,128)(2,1)}, bf16[192,384]{1,0:T(8,128)(2,1)S(1)}, u32[]{:S(2)}, u32[]{:S(2)}) collective-permute-start(bf16[192,384]{1,0:T(8,128)(2,1)} %bitcast.98), channel_id=1, source_target_pairs={{0,2},{1,3},{2,0},{3,1},{4,6},{5,7},{6,4},{7,5},{8,10},{9,11},{10,... | collective-permute-start | bytes 442376 | tf_op jit(solution)/shard_map/ppermute | solution.py:1409
  12.0 13.3 %collective-permute-start = (bf16[192,384]{1,0:T(8,128)(2,1)}, bf16[192,384]{1,0:T(8,128)(2,1)S(1)}, u32[]{:S(2)}, u32[]{:S(2)}) collective-permute-start(bf16[192,384]{1,0:T(8,128)(2,1)} %bitcast.99), channel_id=1, source_target_pairs={{0,1},{1,2},{2,3},{3,0},{4,5},{5,6},{6,7},{7,4},{8,9},{9,10},{10,1... | collective-permute-start | bytes 442376 | tf_op jit(solution)/shard_map/ppermute | solution.py:1409
  13.6 12.4 %collective-permute-start.2 = (bf16[192,384]{1,0:T(8,128)(2,1)}, bf16[192,384]{1,0:T(8,128)(2,1)S(1)}, u32[]{:S(2)}, u32[]{:S(2)}) collective-permute-start(bf16[192,384]{1,0:T(8,128)(2,1)} %bitcast.100), channel_id=1, source_target_pairs={{0,3},{1,0},{2,1},{3,2},{4,7},{5,4},{6,5},{7,6},{8,11},{9,8},{10,9... | collective-permute-start | bytes 442376 | tf_op jit(solution)/shard_map/ppermute | solution.py:1409
  17.2 39.4 %all-to-all-start = ((f32[32,1,128]{2,1,0:T(1,128)}), f32[32,1,128]{2,1,0:T(1,128)S(1)}, u32[]{:S(2)}, u32[]{:S(2)}) async-start(f32[32,1,128]{2,1,0:T(1,128)} %broadcast_in_dim.47), calls=%async_computation | async-start | bytes 32768 | tf_op jit(solution)/shard_map/all_to_all | solution.py:1458
  26.1 9.8 %collective-permute-start.4 = (bf16[2,192,384]{2,1,0:T(8,128)(2,1)S(1)}, bf16[2,192,384]{2,1,0:T(8,128)(2,1)S(1)}, u32[]{:S(2)}, u32[]{:S(2)}) collective-permute-start(bf16[2,192,384]{2,1,0:T(8,128)(2,1)S(1)} %maximum_bitcast_fusion), channel_id=1, source_target_pairs={{0,16},{16,0},{1,17},{17,1},{2,18},{18,2},{3,19},{19,3},{4,20},{20... | collective-permute-start | bytes 884744 | tf_op jit(solution)/shard_map/ppermute | solution.py:1404
  27.5 9.8 %collective-permute-start.3 = (bf16[2,192,384]{2,1,0:T(8,128)(2,1)S(1)}, bf16[2,192,384]{2,1,0:T(8,128)(2,1)S(1)}, u32[]{:S(2)}, u32[]{:S(2)}) collective-permute-start(bf16[2,192,384]{2,1,0:T(8,128)(2,1)S(1)} %maximum_bitcast_fusion), channel_id=1, source_target_pairs={{0,8},{8,0},{1,9},{9,1},{2,10},{10,2},{3,11},{11,3},{4,12},{12,4},... | collective-permute-start | bytes 884744 | tf_op jit(solution)/shard_map/ppermute | solution.py:1404
  34.6 22.1 %collective-permute-start.9 = (bf16[4,192,384]{2,1,0:T(8,128)(2,1)S(1)}, bf16[4,192,384]{2,1,0:T(8,128)(2,1)S(1)}, u32[]{:S(2)}, u32[]{:S(2)}) collective-permute-start(bf16[4,192,384]{2,1,0:T(8,128)(2,1)S(1)} %pad_maximum_fusion.1), channel_id=1, source_target_pairs={{0,16},{16,0},{1,17},{17,1},{2,18},{18,2},{3,19},{19,3},{4,20},{20... | collective-permute-start | bytes 1769480 | tf_op jit(solution)/shard_map/ppermute | solution.py:1404
  35.2 21.5 %collective-permute-start.8 = (bf16[4,192,384]{2,1,0:T(8,128)(2,1)S(1)}, bf16[4,192,384]{2,1,0:T(8,128)(2,1)}, u32[]{:S(2)}, u32[]{:S(2)}) collective-permute-start(bf16[4,192,384]{2,1,0:T(8,128)(2,1)S(1)} %pad_maximum_fusion.1), channel_id=1, source_target_pairs={{0,8},{8,0},{1,9},{9,1},{2,10},{10,2},{3,11},{11,3},{4,12},{12,4},... | collective-permute-start | bytes 1769480 | tf_op jit(solution)/shard_map/ppermute | solution.py:1404
  35.9 16.7 %collective-permute-start.5 = (bf16[1,192,384]{2,1,0:T(8,128)(2,1)S(1)}, bf16[1,192,384]{2,1,0:T(8,128)(2,1)S(1)}, u32[]{:S(2)}, u32[]{:S(2)}) collective-permute-start(bf16[1,192,384]{2,1,0:T(8,128)(2,1)S(1)} %slice.235), channel_id=1, source_target_pairs={{0,8},{8,0},{1,9},{9,1},{2,10},{10,2},{3,11},{11,3},{4,12},{12,4},... | collective-permute-start | bytes 442376 | tf_op jit(solution)/shard_map/ppermute | solution.py:1404
  37.3 15.3 %collective-permute-start.6 = (bf16[1,192,384]{2,1,0:T(8,128)(2,1)S(1)}, bf16[1,192,384]{2,1,0:T(8,128)(2,1)S(1)}, u32[]{:S(2)}, u32[]{:S(2)}) collective-permute-start(bf16[1,192,384]{2,1,0:T(8,128)(2,1)S(1)} %slice.236), channel_id=1, source_target_pairs={{0,16},{16,0},{1,17},{17,1},{2,18},{18,2},{3,19},{19,3},{4,20},{20... | collective-permute-start | bytes 442376 | tf_op jit(solution)/shard_map/ppermute | solution.py:1404
  52.7 11.8 %collective-permute-start.7 = (bf16[8,192,384]{2,1,0:T(8,128)(2,1)S(1)}, bf16[8,192,384]{2,1,0:T(8,128)(2,1)}, u32[]{:S(2)}, u32[]{:S(2)}) collective-permute-start(bf16[8,192,384]{2,1,0:T(8,128)(2,1)S(1)} %constant_dynamic-update-slice_fusion.mine_ref), channel_id=1, source_target_pairs={{0,4},{4,0},{1,5},{5,1},{2,6},{6,2},{3,7},{7,3},{8,12},{12,8},{9,1... | collective-permute-start | bytes 3538952 | tf_op jit(solution)/shard_map/ppermute | solution.py:1404
  60.1 21.1 %all-to-all-start.1 = ((bf16[8,192,384]{2,1,0:T(8,128)(2,1)}), bf16[8,192,384]{2,1,0:T(8,128)(2,1)}, u32[]{:S(2)}, u32[]{:S(2)}) async-start(bf16[8,192,384]{2,1,0:T(8,128)(2,1)} %cut_units.1), calls=%async_computation.1 | async-start | bytes 2359296 | tf_op jit(solution)/shard_map/all_to_all | solution.py:1458
  64.4 136.7 %all-gather.5.cloned.1.call-start = ((), (), s32[]{:S(2)}) async-start(), calls=%async_computation.11 | async-start | bytes 5898240 | tf_op jit(solution)/shard_map/all_gather | solution.py:1513
  83.4 11.9 %collective-permute-start.11 = (bf16[2,192,384]{2,1,0:T(8,128)(2,1)S(1)}, bf16[2,192,384]{2,1,0:T(8,128)(2,1)S(1)}, u32[]{:S(2)}, u32[]{:S(2)}) collective-permute-start(bf16[2,192,384]{2,1,0:T(8,128)(2,1)S(1)} %slice.186), channel_id=1, source_target_pairs={{0,16},{16,0},{1,17},{17,1},{2,18},{18,2},{3,19},{19,3},{4,20},{20... | collective-permute-start | bytes 884744 | tf_op jit(solution)/shard_map/ppermute | solution.py:1404
  84.0 11.3 %collective-permute-start.10 = (bf16[2,192,384]{2,1,0:T(8,128)(2,1)S(1)}, bf16[2,192,384]{2,1,0:T(8,128)(2,1)S(1)}, u32[]{:S(2)}, u32[]{:S(2)}) collective-permute-start(bf16[2,192,384]{2,1,0:T(8,128)(2,1)S(1)} %slice.185), channel_id=1, source_target_pairs={{0,8},{8,0},{1,9},{9,1},{2,10},{10,2},{3,11},{11,3},{4,12},{12,4},... | collective-permute-start | bytes 884744 | tf_op jit(solution)/shard_map/ppermute | solution.py:1404
  95.2 23.6 %all-to-all-start.2 = ((bf16[4,512,384]{2,1,0:T(8,128)(2,1)}), bf16[4,512,384]{2,1,0:T(8,128)(2,1)S(1)}, u32[]{:S(2)}, u32[]{:S(2)}) async-start(bf16[4,512,384]{2,1,0:T(8,128)(2,1)} %get-tuple-element.116), calls=%async_computation.2 | async-start | bytes 3145728 | tf_op jit(solution)/shard_map/all_to_all | solution.py:1458
  104.2 53.2 %collective-permute-start.14 = (bf16[16,192,384]{2,1,0:T(8,128)(2,1)}, bf16[16,192,384]{2,1,0:T(8,128)(2,1)}, u32[]{:S(2)}, u32[]{:S(2)}) collective-permute-start(bf16[16,192,384]{2,1,0:T(8,128)(2,1)} %constant_dynamic-update-slice_fusion.5.mine_ref), channel_id=1, source_target_pairs={{0,4},{4,0},{1,5},{5,1},{2,6},{6,2},{3,7},{7,3},{8,12},{12,8},{9,1... | collective-permute-start | bytes 7077896 | tf_op jit(solution)/shard_map/ppermute | solution.py:1404
  118.9 22.0 %collective-permute-start.13 = (bf16[256,1536]{1,0:T(8,128)(2,1)S(1)}, bf16[256,1536]{1,0:T(8,128)(2,1)S(1)}, u32[]{:S(2)}, u32[]{:S(2)}) collective-permute-start(bf16[256,1536]{1,0:T(8,128)(2,1)S(1)} %bitcast.81), channel_id=1, source_target_pairs={{0,16},{16,0},{1,17},{17,1},{2,18},{18,2},{3,19},{19,3},{4,20},{20... | collective-permute-start | bytes 2359304 | tf_op jit(solution)/shard_map/ppermute | solution.py:1404
  120.3 20.6 %collective-permute-start.12 = (bf16[256,1536]{1,0:T(8,128)(2,1)S(1)}, bf16[256,1536]{1,0:T(8,128)(2,1)S(1)}, u32[]{:S(2)}, u32[]{:S(2)}) collective-permute-start(bf16[256,1536]{1,0:T(8,128)(2,1)S(1)} %bitcast.82), channel_id=1, source_target_pairs={{0,8},{8,0},{1,9},{9,1},{2,10},{10,2},{3,11},{11,3},{4,12},{12,4},... | collective-permute-start | bytes 2359304 | tf_op jit(solution)/shard_map/ppermute | solution.py:1404
  142.7 52.3 %all-to-all-start.3 = ((bf16[16,64,384]{2,1,0:T(8,128)(2,1)}), bf16[16,64,384]{2,1,0:T(8,128)(2,1)S(1)}, u32[]{:S(2)}, u32[]{:S(2)}) async-start(bf16[16,64,384]{2,1,0:T(8,128)(2,1)} %get-tuple-element.119), calls=%async_computation.3 | async-start | bytes 1572864 | tf_op jit(solution)/shard_map/all_to_all | solution.py:1458
  157.3 248.5 %reduce-scatter.3.cloned.1.call-start = ((), (), s32[]{:S(2)}) async-start(), calls=%async_computation.12 | async-start | bytes 5898240 | tf_op jit(solution)/shard_map/reduce_scatter | solution.py:1551
  162.5 11.5 %collective-permute-start.16 = (bf16[128,1536]{1,0:T(8,128)(2,1)S(1)}, bf16[128,1536]{1,0:T(8,128)(2,1)S(1)}, u32[]{:S(2)}, u32[]{:S(2)}) collective-permute-start(bf16[128,1536]{1,0:T(8,128)(2,1)S(1)} %slice.188), channel_id=1, source_target_pairs={{0,16},{16,0},{1,17},{17,1},{2,18},{18,2},{3,19},{19,3},{4,20},{20... | collective-permute-start | bytes 1179656 | tf_op jit(solution)/shard_map/ppermute | solution.py:1404
  163.3 14.7 %collective-permute-start.15 = (bf16[128,1536]{1,0:T(8,128)(2,1)S(1)}, bf16[128,1536]{1,0:T(8,128)(2,1)S(1)}, u32[]{:S(2)}, u32[]{:S(2)}) collective-permute-start(bf16[128,1536]{1,0:T(8,128)(2,1)S(1)} %slice.187), channel_id=1, source_target_pairs={{0,8},{8,0},{1,9},{9,1},{2,10},{10,2},{3,11},{11,3},{4,12},{12,4},... | collective-permute-start | bytes 1179656 | tf_op jit(solution)/shard_map/ppermute | solution.py:1404
  201.1 20.0 %collective-permute-start.18 = (bf16[256,1536]{1,0:T(8,128)(2,1)S(1)}, bf16[256,1536]{1,0:T(8,128)(2,1)S(1)}, u32[]{:S(2)}, u32[]{:S(2)}) collective-permute-start(bf16[256,1536]{1,0:T(8,128)(2,1)S(1)} %get-tuple-element.129.refs_0_), channel_id=1, source_target_pairs={{0,16},{16,0},{1,17},{17,1},{2,18},{18,2},{3,19},{19,3},{4,20},{20... | collective-permute-start | bytes 2359304 | tf_op jit(solution)/shard_map/ppermute | solution.py:1404
  202.6 19.8 %collective-permute-start.17 = (bf16[256,1536]{1,0:T(8,128)(2,1)S(1)}, bf16[256,1536]{1,0:T(8,128)(2,1)}, u32[]{:S(2)}, u32[]{:S(2)}) collective-permute-start(bf16[256,1536]{1,0:T(8,128)(2,1)S(1)} %get-tuple-element.129.refs_0_), channel_id=1, source_target_pairs={{0,8},{8,0},{1,9},{9,1},{2,10},{10,2},{3,11},{11,3},{4,12},{12,4},... | collective-permute-start | bytes 2359304 | tf_op jit(solution)/shard_map/ppermute | solution.py:1404
  223.4 24.3 %collective-permute-start.20 = (bf16[128,1536]{1,0:T(8,128)(2,1)S(1)}, bf16[128,1536]{1,0:T(8,128)(2,1)S(1)}, u32[]{:S(2)}, u32[]{:S(2)}) collective-permute-start(bf16[128,1536]{1,0:T(8,128)(2,1)S(1)} %slice.190), channel_id=1, source_target_pairs={{0,8},{8,0},{1,9},{9,1},{2,10},{10,2},{3,11},{11,3},{4,12},{12,4},... | collective-permute-start | bytes 1179656 | tf_op jit(solution)/shard_map/ppermute | solution.py:1404
  224.0 23.6 %collective-permute-start.21 = (bf16[128,1536]{1,0:T(8,128)(2,1)S(1)}, bf16[128,1536]{1,0:T(8,128)(2,1)}, u32[]{:S(2)}, u32[]{:S(2)}) collective-permute-start(bf16[128,1536]{1,0:T(8,128)(2,1)S(1)} %slice.191), channel_id=1, source_target_pairs={{0,16},{16,0},{1,17},{17,1},{2,18},{18,2},{3,19},{19,3},{4,20},{20... | collective-permute-start | bytes 1179656 | tf_op jit(solution)/shard_map/ppermute | solution.py:1404
  244.6 34.0 %collective-permute-start.22 = (bf16[128,1536]{1,0:T(8,128)(2,1)}, bf16[128,1536]{1,0:T(8,128)(2,1)S(1)}, u32[]{:S(2)}, u32[]{:S(2)}) collective-permute-start(bf16[128,1536]{1,0:T(8,128)(2,1)} %get-tuple-element.140), channel_id=1, source_target_pairs={{0,8},{8,0},{1,9},{9,1},{2,10},{10,2},{3,11},{11,3},{4,12},{12,4},... | collective-permute-start | bytes 1179656 | tf_op jit(solution)/shard_map/ppermute | solution.py:1404
  246.2 32.5 %collective-permute-start.23 = (bf16[128,1536]{1,0:T(8,128)(2,1)}, bf16[128,1536]{1,0:T(8,128)(2,1)S(1)}, u32[]{:S(2)}, u32[]{:S(2)}) collective-permute-start(bf16[128,1536]{1,0:T(8,128)(2,1)} %get-tuple-element.141), channel_id=1, source_target_pairs={{0,16},{16,0},{1,17},{17,1},{2,18},{18,2},{3,19},{19,3},{4,20},{20... | collective-permute-start | bytes 1179656 | tf_op jit(solution)/shard_map/ppermute | solution.py:1404
  258.2 20.4 %collective-permute-start.24 = (bf16[128,1536]{1,0:T(8,128)(2,1)}, bf16[128,1536]{1,0:T(8,128)(2,1)S(1)}, u32[]{:S(2)}, u32[]{:S(2)}) collective-permute-start(bf16[128,1536]{1,0:T(8,128)(2,1)} %get-tuple-element.142), channel_id=1, source_target_pairs={{0,8},{8,0},{1,9},{9,1},{2,10},{10,2},{3,11},{11,3},{4,12},{12,4},... | collective-permute-start | bytes 1179656 | tf_op jit(solution)/shard_map/ppermute | solution.py:1404
  258.8 19.8 %collective-permute-start.25 = (bf16[128,1536]{1,0:T(8,128)(2,1)}, bf16[128,1536]{1,0:T(8,128)(2,1)S(1)}, u32[]{:S(2)}, u32[]{:S(2)}) collective-permute-start(bf16[128,1536]{1,0:T(8,128)(2,1)} %get-tuple-element.143), channel_id=1, source_target_pairs={{0,16},{16,0},{1,17},{17,1},{2,18},{18,2},{3,19},{19,3},{4,20},{20... | collective-permute-start | bytes 1179656 | tf_op jit(solution)/shard_map/ppermute | solution.py:1404
  280.3 12.1 %collective-permute-start.28 = (bf16[128,1536]{1,0:T(8,128)(2,1)S(1)}, bf16[128,1536]{1,0:T(8,128)(2,1)S(1)}, u32[]{:S(2)}, u32[]{:S(2)}) collective-permute-start(bf16[128,1536]{1,0:T(8,128)(2,1)S(1)} %get-tuple-element.230), channel_id=1, source_target_pairs={{0,16},{16,0},{1,17},{17,1},{2,18},{18,2},{3,19},{19,3},{4,20},{20... | collective-permute-start | bytes 1179656 | tf_op jit(solution)/shard_map/ppermute | solution.py:1404
  281.8 11.2 %collective-permute-start.27 = (bf16[128,1536]{1,0:T(8,128)(2,1)S(1)}, bf16[128,1536]{1,0:T(8,128)(2,1)S(1)}, u32[]{:S(2)}, u32[]{:S(2)}) collective-permute-start(bf16[128,1536]{1,0:T(8,128)(2,1)S(1)} %get-tuple-element.231), channel_id=1, source_target_pairs={{0,8},{8,0},{1,9},{9,1},{2,10},{10,2},{3,11},{11,3},{4,12},{12,4},... | collective-permute-start | bytes 1179656 | tf_op jit(solution)/shard_map/ppermute | solution.py:1404
  307.9 20.1 %collective-permute-start.29 = (bf16[8,96,1536]{2,1,0:T(8,128)(2,1)}, bf16[8,96,1536]{2,1,0:T(8,128)(2,1)}, u32[]{:S(2)}, u32[]{:S(2)}) collective-permute-start(bf16[8,96,1536]{2,1,0:T(8,128)(2,1)} %get-tuple-element.166), channel_id=1, source_target_pairs={{0,4},{4,0},{1,5},{5,1},{2,6},{6,2},{3,7},{7,3},{8,12},{12,8},{9,1... | collective-permute-start | bytes 7077896 | tf_op jit(solution)/shard_map/ppermute | solution.py:1404
  307.9 45.3 %all-to-all-start.4 = ((bf16[16,64,384]{2,1,0:T(8,128)(2,1)}), bf16[16,64,384]{2,1,0:T(8,128)(2,1)}, u32[]{:S(2)}, u32[]{:S(2)}) async-start(bf16[16,64,384]{2,1,0:T(8,128)(2,1)} %copy-done.6), calls=%async_computation.4 | async-start | bytes 1572864 | tf_op jit(solution)/shard_map/all_to_all | solution.py:1458
  325.7 56.5 %collective-permute-start.31 = (bf16[256,1536]{1,0:T(8,128)(2,1)}, bf16[256,1536]{1,0:T(8,128)(2,1)}, u32[]{:S(2)}, u32[]{:S(2)}) collective-permute-start(bf16[256,1536]{1,0:T(8,128)(2,1)} %get-tuple-element.167), channel_id=1, source_target_pairs={{0,8},{8,0},{1,9},{9,1},{2,10},{10,2},{3,11},{11,3},{4,12},{12,4},... | collective-permute-start | bytes 2359304 | tf_op jit(solution)/shard_map/ppermute | solution.py:1404
  327.3 54.9 %collective-permute-start.32 = (bf16[256,1536]{1,0:T(8,128)(2,1)}, bf16[256,1536]{1,0:T(8,128)(2,1)}, u32[]{:S(2)}, u32[]{:S(2)}) collective-permute-start(bf16[256,1536]{1,0:T(8,128)(2,1)} %get-tuple-element.168), channel_id=1, source_target_pairs={{0,16},{16,0},{1,17},{17,1},{2,18},{18,2},{3,19},{19,3},{4,20},{20... | collective-permute-start | bytes 2359304 | tf_op jit(solution)/shard_map/ppermute | solution.py:1404
  332.6 49.5 %collective-permute-start.30 = (bf16[384,1536]{1,0:T(8,128)(2,1)S(1)}, bf16[384,1536]{1,0:T(8,128)(2,1)S(1)}, u32[]{:S(2)}, u32[]{:S(2)}) collective-permute-start(bf16[384,1536]{1,0:T(8,128)(2,1)S(1)} %bitcast.93), channel_id=1, source_target_pairs={{0,8},{8,0},{1,9},{9,1},{2,10},{10,2},{3,11},{11,3},{4,12},{12,4},... | collective-permute-start | bytes 3538952 | tf_op jit(solution)/shard_map/ppermute | solution.py:1404
  382.2 23.6 %all-to-all-start.5 = ((bf16[4,512,384]{2,1,0:T(8,128)(2,1)}), bf16[4,512,384]{2,1,0:T(8,128)(2,1)S(1)}, u32[]{:S(2)}, u32[]{:S(2)}) async-start(bf16[4,512,384]{2,1,0:T(8,128)(2,1)} %bitcast.90), calls=%async_computation.5 | async-start | bytes 3145728 | tf_op jit(solution)/shard_map/all_to_all | solution.py:1458
  385.7 97.1 %reduce-scatter.5.cloned.1.call-start = ((), (), s32[]{:S(2)}) async-start(), calls=%async_computation.13 | async-start | bytes 4669440 | tf_op jit(solution)/shard_map/reduce_scatter | solution.py:1575
  387.8 15.7 %collective-permute-start.35 = (bf16[192,1536]{1,0:T(8,128)(2,1)S(1)}, bf16[192,1536]{1,0:T(8,128)(2,1)S(1)}, u32[]{:S(2)}, u32[]{:S(2)}) collective-permute-start(bf16[192,1536]{1,0:T(8,128)(2,1)S(1)} %slice.296), channel_id=1, source_target_pairs={{0,16},{16,0},{1,17},{17,1},{2,18},{18,2},{3,19},{19,3},{4,20},{20... | collective-permute-start | bytes 1769480 | tf_op jit(solution)/shard_map/ppermute | solution.py:1404
  415.9 12.1 %collective-permute-start.33 = (bf16[128,1536]{1,0:T(8,128)(2,1)S(1)}, bf16[128,1536]{1,0:T(8,128)(2,1)S(1)}, u32[]{:S(2)}, u32[]{:S(2)}) collective-permute-start(bf16[128,1536]{1,0:T(8,128)(2,1)S(1)} %add_convert_fusion.2), channel_id=1, source_target_pairs={{0,16},{16,0},{1,17},{17,1},{2,18},{18,2},{3,19},{19,3},{4,20},{20... | collective-permute-start | bytes 1179656 | tf_op jit(solution)/shard_map/ppermute | solution.py:1404
  417.7 22.5 %all-to-all-start.6 = ((bf16[8,192,384]{2,1,0:T(8,128)(2,1)}), bf16[8,192,384]{2,1,0:T(8,128)(2,1)}, u32[]{:S(2)}, u32[]{:S(2)}) async-start(bf16[8,192,384]{2,1,0:T(8,128)(2,1)} %bitcast.38), calls=%async_computation.8 | async-start | bytes 2359296 | tf_op jit(solution)/shard_map/all_to_all | solution.py:1458
  430.8 15.5 %collective-permute-start.34 = (bf16[128,1536]{1,0:T(8,128)(2,1)}, bf16[128,1536]{1,0:T(8,128)(2,1)}, u32[]{:S(2)}, u32[]{:S(2)}) collective-permute-start(bf16[128,1536]{1,0:T(8,128)(2,1)} %get-tuple-element.229), channel_id=1, source_target_pairs={{0,8},{8,0},{1,9},{9,1},{2,10},{10,2},{3,11},{11,3},{4,12},{12,4},... | collective-permute-start | bytes 1179656 | tf_op jit(solution)/shard_map/ppermute | solution.py:1404
  440.1 9.1 %collective-permute-start.36 = (bf16[8,96,768]{2,1,0:T(8,128)(2,1)}, bf16[8,96,768]{2,1,0:T(8,128)(2,1)}, u32[]{:S(2)}, u32[]{:S(2)}) collective-permute-start(bf16[8,96,768]{2,1,0:T(8,128)(2,1)} %copy-done.9), channel_id=1, source_target_pairs={{0,4},{4,0},{1,5},{5,1},{2,6},{6,2},{3,7},{7,3},{8,12},{12,8},{9,1... | collective-permute-start | bytes 3538952 | tf_op jit(solution)/shard_map/ppermute | solution.py:1404
  453.2 8.9 %collective-permute-start.37 = (bf16[192,768]{1,0:T(8,128)(2,1)}, bf16[192,768]{1,0:T(8,128)(2,1)S(1)}, u32[]{:S(2)}, u32[]{:S(2)}) collective-permute-start(bf16[192,768]{1,0:T(8,128)(2,1)} %bitcast.41), channel_id=1, source_target_pairs={{0,8},{8,0},{1,9},{9,1},{2,10},{10,2},{3,11},{11,3},{4,12},{12,4},... | collective-permute-start | bytes 884744 | tf_op jit(solution)/shard_map/ppermute | solution.py:1404
  470.1 10.9 %all-to-all-start.7 = ((f32[32,1,128]{2,1,0:T(1,128)}), f32[32,1,128]{2,1,0:T(1,128)S(1)}, u32[]{:S(2)}, u32[]{:S(2)}) async-start(f32[32,1,128]{2,1,0:T(1,128)} %bitcast.45), calls=%async_computation.9 | async-start | bytes 32768 | tf_op jit(solution)/shard_map/all_to_all | solution.py:1458
  (52 other events, 609.0 us)
Sparse Core Ops, SparseCore 0:
  9.6 67.6 all-gather.2
  81.3 113.7 all-gather.4
  294.0 95.3 reduce-scatter.2
  414.7 68.1 reduce-scatter.4
